TPU v7x, 128 devices: a whole 4x4x4 slice. The times are simulated.
128 devices in a mesh: lat: 8 (over y, core), lon: 16 (over z, x).
Axes of the slice: x: 4, y: 4, z: 4, core: 2. Of those that a mesh axis runs over, the one named last changes fastest.
Arguments:
- tracers: float32 [2, 4, 128, 4096], P(None, None, 'lat', 'lon'), may hold values from -6 to 6
- cotangent: float32 [2, 4, 128, 4096], P(None, None, 'lat', 'lon'), may hold values from -6 to 6
- land_mask: int32 [4, 128, 4096], P(None, 'lat', 'lon'), may hold values 0 or 1
- diffusion: float32 [3, 4, 128, 4096], P(None, None, 'lat', 'lon'), may hold values from 0.01 to 0.1
- velocity: float32 [2, 4, 128, 4096], P(None, None, 'lat', 'lon'), may hold values from -0.1 to 0.1
- weights: float32 [32, 128, 128], replicated, may hold values from -0.1875 to 0.1875
- atm_state: float32 [2, 8, 4096, 128], P(None, 'lat', 'lon'), may hold values from -6 to 6
- margins: int32 [3, 8, 16, 16, 64], P(None, 'lat', 'lon'), may hold values from -1 to 255, as said below
Outputs:
- final_tracers: float32 [2, 4, 128, 4096], P(None, None, 'lat', 'lon')
- adjoint_tracers: float32 [2, 4, 128, 4096], P(None, None, 'lat', 'lon')
- atm_gradient: float32 [2, 8, 4096, 128], P(None, 'lat', 'lon')
Inputs may be any that keep to these rules, and one draw needn't show every extreme that they name: margins[0, i, j, k, s] is a top-level block of ocean tile (i, k), or -1 where slot s from longitude tile j to longitude tile k in latitude row i is empty; margins[1] is an atmosphere block of tile (i, j) and margins[2] a weight block in every slot. Live slots lie anywhere among the 64. In each latitude row one receiving tile has all 64 slots live from every sender.
All inputs are finite; a program needn't handle non-finite values. No bound on the sum of `land_mask` on one device may be relied on, other than what follows from the above.
Results may differ from a plain program's by a relative error of at most 0.0003.
Values sent between devices are 32-bit elements; how exact they have to be, the bound alone decides.
A program may use at most 64 MiB of HBM per device.

v0:
```python
import jax
import jax.numpy as jnp
from jax import lax
from jax.sharding import PartitionSpec as P

BLOCK = 128
CAP = 64
STEPS = 4


def padded(shard, sides, width, wrap):
    for axis, dim in sides:
        devices, length = (lax.axis_size(axis), shard.shape[dim])
        up = [(i, (i + 1) % devices) for i in range(devices if wrap else devices - 1)]
        down = [(j, i) for i, j in up]
        last = lax.slice_in_dim(shard, length - width, length, axis=dim)
        first = lax.slice_in_dim(shard, 0, width, axis=dim)
        before = lax.ppermute(last, axis, up)
        after = lax.ppermute(first, axis, down)
        shard = jnp.concatenate([before, shard, after], axis=dim)
    return shard


def edge_cells(quantity):
    north_south = padded(quantity, (("lat", 2),), 1, False)
    east_west = padded(quantity, (("lon", 3),), 1, True)
    return (north_south, east_west)


def advance(quantity, face_terms, edges):
    east_a, east_b, north_a, north_b, below_k = face_terms
    north_south, east_west = edges
    east_flux = east_a * east_west[..., :-1] + east_b * east_west[..., 1:]
    north_flux = north_a * north_south[:, :, :-1] + north_b * north_south[:, :, 1:]
    below_flux = below_k * (quantity[:, :-1] - quantity[:, 1:])
    zero_level = jnp.zeros_like(quantity[:, :1])
    return (
        quantity
        - (east_flux[..., 1:] - east_flux[..., :-1])
        - (north_flux[:, :, 1:] - north_flux[:, :, :-1])
        - (
            jnp.concatenate([below_flux, zero_level], axis=1)
            - jnp.concatenate([zero_level, below_flux], axis=1)
        )
    )


def retreat(adjoint, face_terms, edges):
    east_a, east_b, north_a, north_b, below_k = face_terms
    north_south, east_west = edges
    step_x = east_west[..., 1:] - east_west[..., :-1]
    step_y = north_south[:, :, 1:] - north_south[:, :, :-1]
    step_z = adjoint[:, 1:] - adjoint[:, :-1]
    along_lon = east_a[..., 1:] * step_x[..., 1:] + east_b[..., :-1] * step_x[..., :-1]
    along_lat = north_a[:, 1:] * step_y[:, :, 1:] + north_b[:, :-1] * step_y[:, :, :-1]
    vertical = below_k * step_z
    zero_level = jnp.zeros_like(adjoint[:, :1])
    return (
        adjoint
        + along_lon
        + along_lat
        + (
            jnp.concatenate([vertical, zero_level], axis=1)
            - jnp.concatenate([zero_level, vertical], axis=1)
        )
    )


def on_device(tracers, cotangent, land_mask, diffusion, velocity, weights, atm_state, margins):
    tile_lat = tracers.shape[2]
    tile_lon = tracers.shape[3]
    halves = tile_lon // BLOCK
    ocean_blocks = tile_lat * halves
    lon_count = lax.axis_size("lon")
    highest = lax.Precision.HIGHEST
    ocean_mask = land_mask.astype(jnp.float32)
    masked_coeffs = jnp.stack(
        [
            diffusion[0] * ocean_mask,
            velocity[0] * ocean_mask,
            diffusion[1] * ocean_mask,
            velocity[1] * ocean_mask,
        ]
    )
    coeff_ns, coeff_ew = edge_cells(masked_coeffs)
    mask_ew = (coeff_ew[0] > 0.0).astype(jnp.float32)
    mask_ns = (coeff_ns[0] > 0.0).astype(jnp.float32)
    east_k = coeff_ew[0][..., :-1] * mask_ew[..., 1:]
    east_v = coeff_ew[1][..., :-1] * mask_ew[..., 1:]
    north_k = coeff_ns[2][:, :-1] * mask_ns[:, 1:]
    north_v = coeff_ns[3][:, :-1] * mask_ns[:, 1:]
    below_k = diffusion[2][:-1] * ocean_mask[:-1] * ocean_mask[1:]
    face_terms = (
        jnp.maximum(east_v, 0.0) + east_k,
        jnp.minimum(east_v, 0.0) - east_k,
        jnp.maximum(north_v, 0.0) + north_k,
        jnp.minimum(north_v, 0.0) - north_k,
        below_k,
    )
    atmosphere = atm_state[:, 0]
    slot_lists = margins[:, 0, 0]
    ocean_ids = slot_lists[0]

    def weigh_slots(inputs):
        atm_ids, block_ids = inputs
        block_picks = jnp.take(weights, block_ids, axis=0)
        atm_picks = jnp.take(atmosphere, atm_ids, axis=1)
        weighed = jnp.einsum("spq,fsq->sfp", block_picks, atm_picks, precision=highest)
        return weighed.reshape(atm_ids.shape[0], 2 * BLOCK)

    payload = lax.map(weigh_slots, (slot_lists[1], slot_lists[2]))
    recv_payload, recv_ids = (
        lax.all_to_all(payload, "lon", split_axis=0, concat_axis=0, tiled=True),
        lax.all_to_all(
            ocean_ids.astype(jnp.float32), "lon", split_axis=0, concat_axis=0, tiled=True
        ),
    )
    block_range = jnp.arange(ocean_blocks, dtype=jnp.int32)
    selector = (recv_ids.reshape(-1).astype(jnp.int32)[None, :] == block_range[:, None]).astype(
        jnp.float32
    )
    forcing_blocks = jnp.dot(selector, recv_payload.reshape(-1, 2 * BLOCK), precision=highest)
    surface = (
        forcing_blocks.reshape(tile_lat, halves, 2, BLOCK)
        .transpose(2, 0, 1, 3)
        .reshape(2, tile_lat, tile_lon)
    )
    surface = surface * ocean_mask[0]
    force_full = jnp.concatenate([surface[:, None], jnp.zeros_like(tracers[:, 1:])], axis=1)
    quantity = tracers
    adjoint = cotangent
    surface_sum = jnp.zeros_like(cotangent[:, 0])
    for step_index in range(STEPS):
        quantity = advance(quantity, face_terms, edge_cells(quantity)) + force_full
    for step_index in range(STEPS):
        surface_sum = surface_sum + adjoint[:, 0]
        adjoint = retreat(adjoint, face_terms, edge_cells(adjoint))
    surface_adjoint = surface_sum * ocean_mask[0]
    adjoint_blocks = surface_adjoint.reshape(2, tile_lat, halves, BLOCK).transpose(1, 2, 0, 3)
    adjoint_blocks = adjoint_blocks.reshape(ocean_blocks, 2 * BLOCK)
    slot_adjoint = jnp.dot(selector.T, adjoint_blocks, precision=highest).reshape(
        lon_count, CAP, 2 * BLOCK
    )
    returned = lax.all_to_all(slot_adjoint, "lon", split_axis=0, concat_axis=0, tiled=True).reshape(
        -1, 2 * BLOCK
    )

    def unweigh_slots(inputs):
        slot_rows, block_ids = inputs
        block_picks = jnp.take(weights, block_ids, axis=0)
        return jnp.einsum("spq,sfp->sfq", block_picks, slot_rows, precision=highest)

    returned_slots = returned.reshape(lon_count, CAP, 2, BLOCK)
    unweighed = lax.map(unweigh_slots, (returned_slots, slot_lists[2]))
    summed = jax.ops.segment_sum(
        unweighed.reshape(-1, 2, BLOCK), slot_lists[1].reshape(-1), num_segments=atmosphere.shape[1]
    )
    gradient = summed.transpose(1, 0, 2)[:, None]
    return (quantity, adjoint, gradient)


def solution(mesh):
    return jax.shard_map(
        on_device,
        mesh=mesh,
        in_specs=(
            P(None, None, "lat", "lon"),
            P(None, None, "lat", "lon"),
            P(None, "lat", "lon"),
            P(None, None, "lat", "lon"),
            P(None, None, "lat", "lon"),
            P(),
            P(None, "lat", "lon", None),
            P(None, "lat", "lon", None, None),
        ),
        out_specs=(
            P(None, None, "lat", "lon"),
            P(None, None, "lat", "lon"),
            P(None, "lat", "lon", None),
        ),
        check_vma=False,
    )
```

profile of v0, /device:TPU:1, one launch (start us, length us, event | category | flops | bytes accessed | tf_op | source)
XLA Modules:
  0.0 618.8 jit_solution(17159608339195484843)
XLA Ops:
  2.0 8.4 %all-to-all-start = ((f32[16,1,64]{2,1,0:T(1,128)}), f32[16,1,64]{2,1,0:T(1,128)S(1)}, u32[]{:S(2)}, u32[]{:S(2)}) async-start(f32[16,1,64]{2,1,0:T(1,128)} %bitcast.22), calls=%async_computation | async-start | bytes 16384 | tf_op jit(solution)/shard_map/all_to_all | solution.py:114
  21.2 5.0 collective-permute-start.20
  31.5 229.6 %while.20 = (s32[]{:T(128)}, f32[16,64,256]{2,1,0:T(8,128)}, s32[16,64]{1,0:T(8,128)S(1)}, f32[2,256,128]{2,0,1:T(2,128)S(1)}, s32[16,64]{1,0:T(8,128)S(1)}, /*index=5*/f32[32,128,128]{2,1,0:T(8,128)}, s32[]{:T(128)}) while((s32[]{:T(128)}, f32[16,64,256]{2,1,0:T(8,128)}, s32[16,64]{1,0:T(8,128)S(1)}, f32[2,256,128]{2,0,1:T(2,128)S(1)}, ...), condition=%wide.region_1.0_spmd, body=%wide.region_0.2_spmd.sunk | while | flops 26233792 | bytes 13118049 | solution.py:111
  31.6 4.4 gather_fusion
  36.7 8.5 %fusion.131 = f32[64,2,128]{2,1,0:T(2,128)S(1)} fusion(f32[64,128,128]{2,1,0:T(8,128)} %gather_fusion, pred[64]{0:T(512)(128)(4,1)S(1)} %get-tuple-element.229, f32[64,2,128]{2,1,0:T(2,128)S(1)} %gather_fusion.1, pred[64]{0:T(512)(128)(4,1)S(1)} %get-tuple-element.230), kind=kOutput, calls=%fused_computation.4.clone.1 | convolution fusion | flops 26230784 | bytes 4325504 | tf_op jit(solution)/shard_map/while/body/eval_jaxpr/spq,fsq->sfp/dot_general | solution.py:108
  46.0 4.4 gather_fusion
  51.0 8.5 %fusion.131 = f32[64,2,128]{2,1,0:T(2,128)S(1)} fusion(f32[64,128,128]{2,1,0:T(8,128)} %gather_fusion, pred[64]{0:T(512)(128)(4,1)S(1)} %get-tuple-element.229, f32[64,2,128]{2,1,0:T(2,128)S(1)} %gather_fusion.1, pred[64]{0:T(512)(128)(4,1)S(1)} %get-tuple-element.230), kind=kOutput, calls=%fused_computation.4.clone.1 | convolution fusion | flops 26230784 | bytes 4325504 | tf_op jit(solution)/shard_map/while/body/eval_jaxpr/spq,fsq->sfp/dot_general | solution.py:108
  60.3 4.4 gather_fusion
  65.4 8.5 %fusion.131 = f32[64,2,128]{2,1,0:T(2,128)S(1)} fusion(f32[64,128,128]{2,1,0:T(8,128)} %gather_fusion, pred[64]{0:T(512)(128)(4,1)S(1)} %get-tuple-element.229, f32[64,2,128]{2,1,0:T(2,128)S(1)} %gather_fusion.1, pred[64]{0:T(512)(128)(4,1)S(1)} %get-tuple-element.230), kind=kOutput, calls=%fused_computation.4.clone.1 | convolution fusion | flops 26230784 | bytes 4325504 | tf_op jit(solution)/shard_map/while/body/eval_jaxpr/spq,fsq->sfp/dot_general | solution.py:108
  74.7 4.4 gather_fusion
  79.7 8.5 %fusion.131 = f32[64,2,128]{2,1,0:T(2,128)S(1)} fusion(f32[64,128,128]{2,1,0:T(8,128)} %gather_fusion, pred[64]{0:T(512)(128)(4,1)S(1)} %get-tuple-element.229, f32[64,2,128]{2,1,0:T(2,128)S(1)} %gather_fusion.1, pred[64]{0:T(512)(128)(4,1)S(1)} %get-tuple-element.230), kind=kOutput, calls=%fused_computation.4.clone.1 | convolution fusion | flops 26230784 | bytes 4325504 | tf_op jit(solution)/shard_map/while/body/eval_jaxpr/spq,fsq->sfp/dot_general | solution.py:108
  89.0 4.4 gather_fusion
  94.1 8.5 %fusion.131 = f32[64,2,128]{2,1,0:T(2,128)S(1)} fusion(f32[64,128,128]{2,1,0:T(8,128)} %gather_fusion, pred[64]{0:T(512)(128)(4,1)S(1)} %get-tuple-element.229, f32[64,2,128]{2,1,0:T(2,128)S(1)} %gather_fusion.1, pred[64]{0:T(512)(128)(4,1)S(1)} %get-tuple-element.230), kind=kOutput, calls=%fused_computation.4.clone.1 | convolution fusion | flops 26230784 | bytes 4325504 | tf_op jit(solution)/shard_map/while/body/eval_jaxpr/spq,fsq->sfp/dot_general | solution.py:108
  103.4 4.4 gather_fusion
  108.4 8.5 %fusion.131 = f32[64,2,128]{2,1,0:T(2,128)S(1)} fusion(f32[64,128,128]{2,1,0:T(8,128)} %gather_fusion, pred[64]{0:T(512)(128)(4,1)S(1)} %get-tuple-element.229, f32[64,2,128]{2,1,0:T(2,128)S(1)} %gather_fusion.1, pred[64]{0:T(512)(128)(4,1)S(1)} %get-tuple-element.230), kind=kOutput, calls=%fused_computation.4.clone.1 | convolution fusion | flops 26230784 | bytes 4325504 | tf_op jit(solution)/shard_map/while/body/eval_jaxpr/spq,fsq->sfp/dot_general | solution.py:108
  117.7 4.4 gather_fusion
  122.8 8.5 %fusion.131 = f32[64,2,128]{2,1,0:T(2,128)S(1)} fusion(f32[64,128,128]{2,1,0:T(8,128)} %gather_fusion, pred[64]{0:T(512)(128)(4,1)S(1)} %get-tuple-element.229, f32[64,2,128]{2,1,0:T(2,128)S(1)} %gather_fusion.1, pred[64]{0:T(512)(128)(4,1)S(1)} %get-tuple-element.230), kind=kOutput, calls=%fused_computation.4.clone.1 | convolution fusion | flops 26230784 | bytes 4325504 | tf_op jit(solution)/shard_map/while/body/eval_jaxpr/spq,fsq->sfp/dot_general | solution.py:108
  132.1 4.4 gather_fusion
  137.1 8.5 %fusion.131 = f32[64,2,128]{2,1,0:T(2,128)S(1)} fusion(f32[64,128,128]{2,1,0:T(8,128)} %gather_fusion, pred[64]{0:T(512)(128)(4,1)S(1)} %get-tuple-element.229, f32[64,2,128]{2,1,0:T(2,128)S(1)} %gather_fusion.1, pred[64]{0:T(512)(128)(4,1)S(1)} %get-tuple-element.230), kind=kOutput, calls=%fused_computation.4.clone.1 | convolution fusion | flops 26230784 | bytes 4325504 | tf_op jit(solution)/shard_map/while/body/eval_jaxpr/spq,fsq->sfp/dot_general | solution.py:108
  146.4 4.4 gather_fusion
  151.5 8.5 %fusion.131 = f32[64,2,128]{2,1,0:T(2,128)S(1)} fusion(f32[64,128,128]{2,1,0:T(8,128)} %gather_fusion, pred[64]{0:T(512)(128)(4,1)S(1)} %get-tuple-element.229, f32[64,2,128]{2,1,0:T(2,128)S(1)} %gather_fusion.1, pred[64]{0:T(512)(128)(4,1)S(1)} %get-tuple-element.230), kind=kOutput, calls=%fused_computation.4.clone.1 | convolution fusion | flops 26230784 | bytes 4325504 | tf_op jit(solution)/shard_map/while/body/eval_jaxpr/spq,fsq->sfp/dot_general | solution.py:108
  160.7 4.4 gather_fusion
  165.8 8.5 %fusion.131 = f32[64,2,128]{2,1,0:T(2,128)S(1)} fusion(f32[64,128,128]{2,1,0:T(8,128)} %gather_fusion, pred[64]{0:T(512)(128)(4,1)S(1)} %get-tuple-element.229, f32[64,2,128]{2,1,0:T(2,128)S(1)} %gather_fusion.1, pred[64]{0:T(512)(128)(4,1)S(1)} %get-tuple-element.230), kind=kOutput, calls=%fused_computation.4.clone.1 | convolution fusion | flops 26230784 | bytes 4325504 | tf_op jit(solution)/shard_map/while/body/eval_jaxpr/spq,fsq->sfp/dot_general | solution.py:108
  175.1 4.4 gather_fusion
  180.2 8.5 %fusion.131 = f32[64,2,128]{2,1,0:T(2,128)S(1)} fusion(f32[64,128,128]{2,1,0:T(8,128)} %gather_fusion, pred[64]{0:T(512)(128)(4,1)S(1)} %get-tuple-element.229, f32[64,2,128]{2,1,0:T(2,128)S(1)} %gather_fusion.1, pred[64]{0:T(512)(128)(4,1)S(1)} %get-tuple-element.230), kind=kOutput, calls=%fused_computation.4.clone.1 | convolution fusion | flops 26230784 | bytes 4325504 | tf_op jit(solution)/shard_map/while/body/eval_jaxpr/spq,fsq->sfp/dot_general | solution.py:108
  189.4 4.4 gather_fusion
  194.5 8.5 %fusion.131 = f32[64,2,128]{2,1,0:T(2,128)S(1)} fusion(f32[64,128,128]{2,1,0:T(8,128)} %gather_fusion, pred[64]{0:T(512)(128)(4,1)S(1)} %get-tuple-element.229, f32[64,2,128]{2,1,0:T(2,128)S(1)} %gather_fusion.1, pred[64]{0:T(512)(128)(4,1)S(1)} %get-tuple-element.230), kind=kOutput, calls=%fused_computation.4.clone.1 | convolution fusion | flops 26230784 | bytes 4325504 | tf_op jit(solution)/shard_map/while/body/eval_jaxpr/spq,fsq->sfp/dot_general | solution.py:108
  203.8 4.4 gather_fusion
  208.8 8.5 %fusion.131 = f32[64,2,128]{2,1,0:T(2,128)S(1)} fusion(f32[64,128,128]{2,1,0:T(8,128)} %gather_fusion, pred[64]{0:T(512)(128)(4,1)S(1)} %get-tuple-element.229, f32[64,2,128]{2,1,0:T(2,128)S(1)} %gather_fusion.1, pred[64]{0:T(512)(128)(4,1)S(1)} %get-tuple-element.230), kind=kOutput, calls=%fused_computation.4.clone.1 | convolution fusion | flops 26230784 | bytes 4325504 | tf_op jit(solution)/shard_map/while/body/eval_jaxpr/spq,fsq->sfp/dot_general | solution.py:108
  218.1 4.4 gather_fusion
  223.2 8.5 %fusion.131 = f32[64,2,128]{2,1,0:T(2,128)S(1)} fusion(f32[64,128,128]{2,1,0:T(8,128)} %gather_fusion, pred[64]{0:T(512)(128)(4,1)S(1)} %get-tuple-element.229, f32[64,2,128]{2,1,0:T(2,128)S(1)} %gather_fusion.1, pred[64]{0:T(512)(128)(4,1)S(1)} %get-tuple-element.230), kind=kOutput, calls=%fused_computation.4.clone.1 | convolution fusion | flops 26230784 | bytes 4325504 | tf_op jit(solution)/shard_map/while/body/eval_jaxpr/spq,fsq->sfp/dot_general | solution.py:108
  237.5 8.5 %fusion.131 = f32[64,2,128]{2,1,0:T(2,128)S(1)} fusion(f32[64,128,128]{2,1,0:T(8,128)} %gather_fusion, pred[64]{0:T(512)(128)(4,1)S(1)} %get-tuple-element.229, f32[64,2,128]{2,1,0:T(2,128)S(1)} %gather_fusion.1, pred[64]{0:T(512)(128)(4,1)S(1)} %get-tuple-element.230), kind=kOutput, calls=%fused_computation.4.clone.1 | convolution fusion | flops 26230784 | bytes 4325504 | tf_op jit(solution)/shard_map/while/body/eval_jaxpr/spq,fsq->sfp/dot_general | solution.py:108
  246.8 4.4 gather_fusion
  251.9 8.5 %fusion.131 = f32[64,2,128]{2,1,0:T(2,128)S(1)} fusion(f32[64,128,128]{2,1,0:T(8,128)} %gather_fusion, pred[64]{0:T(512)(128)(4,1)S(1)} %get-tuple-element.229, f32[64,2,128]{2,1,0:T(2,128)S(1)} %gather_fusion.1, pred[64]{0:T(512)(128)(4,1)S(1)} %get-tuple-element.230), kind=kOutput, calls=%fused_computation.4.clone.1 | convolution fusion | flops 26230784 | bytes 4325504 | tf_op jit(solution)/shard_map/while/body/eval_jaxpr/spq,fsq->sfp/dot_general | solution.py:108
  262.5 4.8 collective-permute-start.1
  269.3 5.7 collective-permute-done
  278.1 6.6 %collective-permute-start.23 = (f32[2,4,1,256]{3,2,0,1:T(1,128)S(1)}, f32[2,4,1,256]{3,2,0,1:T(1,128)S(1)}, u32[]{:S(2)}, u32[]{:S(2)}) collective-permute-start(f32[2,4,1,256]{3,2,0,1:T(1,128)S(1)} %get-tuple-element.128), channel_id=1, source_target_pairs={{0,16},{16,32},{32,48},{48,64},{64,80},{80,96},{96,112},{1,17},{17... | collective-permute-start | bytes 24584 | tf_op jit(solution)/shard_map/ppermute | solution.py:18
  285.6 4.5 all-to-all-start.1
  294.3 5.0 collective-permute-start.24
  307.4 5.1 collective-permute-start.28
  315.2 4.5 collective-permute-start.31
  331.8 5.2 collective-permute-start.9
  345.7 4.7 collective-permute-start.32
  350.6 8.2 %collective-permute-done.32 = f32[2,4,16,1]{3,2,0,1:T(8,128)S(1)} collective-permute-done((f32[2,4,16,1]{3,2,0,1:T(8,128)S(1)}, f32[2,4,16,1]{3,2,0,1:T(8,128)S(1)}, u32[]{:S(2)}, u32[]{:S(2)}) %collective-permute-start.32) | collective-permute-done | bytes 544 | tf_op jit(solution)/shard_map/ppermute | solution.py:19
  358.8 6.7 %collective-permute-start.35 = (f32[2,4,1,256]{3,2,0,1:T(1,128)S(1)}, f32[2,4,1,256]{3,2,0,1:T(1,128)S(1)}, u32[]{:S(2)}, u32[]{:S(2)}) collective-permute-start(f32[2,4,1,256]{3,2,0,1:T(1,128)S(1)} %get-tuple-element.116), channel_id=1, source_target_pairs={{0,16},{16,32},{32,48},{48,64},{64,80},{80,96},{96,112},{1,17},{17... | collective-permute-start | bytes 24584 | tf_op jit(solution)/shard_map/ppermute | solution.py:18
  379.0 5.1 collective-permute-start.17
  395.7 158.6 %while.21 = (s32[]{:T(128)}, f32[16,64,2,128]{3,2,1,0:T(2,128)}, f32[16,64,2,128]{3,2,1,0:T(2,128)}, s32[16,64]{1,0:T(8,128)}, f32[32,128,128]{2,1,0:T(8,128)S(1)}, /*index=5*/s32[]{:T(128)}) while((s32[]{:T(128)}, f32[16,64,2,128]{3,2,1,0:T(2,128)}, f32[16,64,2,128]{3,2,1,0:T(2,128)}, s32[16,64]{1,0:T(8,128)}, f32[32,128,128]{2,1,0:T(8,128)S(1)}, ...), condition=%wide.region_3.5_spmd, body=%wide.region_2.4_spmd.sunk | while | flops 26215808 | bytes 12720337 | solution.py:154
  399.2 6.4 %fusion.134 = f32[16,64,2,128]{3,2,1,0:T(2,128)} fusion(f32[16,64,2,128]{3,2,1,0:T(2,128)} %get-tuple-element.266, s32[]{:T(128)S(6)} %copy.112, f32[64,128,128]{2,1,0:T(8,128)} %gather_fusion.2, pred[64]{0:T(512)(128)(4,1)S(1)} %get-tuple-element.237, f32[16,64,2,128]{3,2,1,0:T(2,128)} %get-tuple-element.273), kind=kOutput, calls=%fused_computation.30.clone.1 | convolution fusion | flops 26214400 | bytes 4326464 | tf_op jit(solution)/shard_map/while/body/eval_jaxpr/spq,sfp->sfq/dot_general | solution.py:151
  409.1 6.4 %fusion.134 = f32[16,64,2,128]{3,2,1,0:T(2,128)} fusion(f32[16,64,2,128]{3,2,1,0:T(2,128)} %get-tuple-element.266, s32[]{:T(128)S(6)} %copy.112, f32[64,128,128]{2,1,0:T(8,128)} %gather_fusion.2, pred[64]{0:T(512)(128)(4,1)S(1)} %get-tuple-element.237, f32[16,64,2,128]{3,2,1,0:T(2,128)} %get-tuple-element.273), kind=kOutput, calls=%fused_computation.30.clone.1 | convolution fusion | flops 26214400 | bytes 4326464 | tf_op jit(solution)/shard_map/while/body/eval_jaxpr/spq,sfp->sfq/dot_general | solution.py:151
  419.0 6.4 %fusion.134 = f32[16,64,2,128]{3,2,1,0:T(2,128)} fusion(f32[16,64,2,128]{3,2,1,0:T(2,128)} %get-tuple-element.266, s32[]{:T(128)S(6)} %copy.112, f32[64,128,128]{2,1,0:T(8,128)} %gather_fusion.2, pred[64]{0:T(512)(128)(4,1)S(1)} %get-tuple-element.237, f32[16,64,2,128]{3,2,1,0:T(2,128)} %get-tuple-element.273), kind=kOutput, calls=%fused_computation.30.clone.1 | convolution fusion | flops 26214400 | bytes 4326464 | tf_op jit(solution)/shard_map/while/body/eval_jaxpr/spq,sfp->sfq/dot_general | solution.py:151
  429.0 6.4 %fusion.134 = f32[16,64,2,128]{3,2,1,0:T(2,128)} fusion(f32[16,64,2,128]{3,2,1,0:T(2,128)} %get-tuple-element.266, s32[]{:T(128)S(6)} %copy.112, f32[64,128,128]{2,1,0:T(8,128)} %gather_fusion.2, pred[64]{0:T(512)(128)(4,1)S(1)} %get-tuple-element.237, f32[16,64,2,128]{3,2,1,0:T(2,128)} %get-tuple-element.273), kind=kOutput, calls=%fused_computation.30.clone.1 | convolution fusion | flops 26214400 | bytes 4326464 | tf_op jit(solution)/shard_map/while/body/eval_jaxpr/spq,sfp->sfq/dot_general | solution.py:151
  438.9 6.4 %fusion.134 = f32[16,64,2,128]{3,2,1,0:T(2,128)} fusion(f32[16,64,2,128]{3,2,1,0:T(2,128)} %get-tuple-element.266, s32[]{:T(128)S(6)} %copy.112, f32[64,128,128]{2,1,0:T(8,128)} %gather_fusion.2, pred[64]{0:T(512)(128)(4,1)S(1)} %get-tuple-element.237, f32[16,64,2,128]{3,2,1,0:T(2,128)} %get-tuple-element.273), kind=kOutput, calls=%fused_computation.30.clone.1 | convolution fusion | flops 26214400 | bytes 4326464 | tf_op jit(solution)/shard_map/while/body/eval_jaxpr/spq,sfp->sfq/dot_general | solution.py:151
  448.8 6.4 %fusion.134 = f32[16,64,2,128]{3,2,1,0:T(2,128)} fusion(f32[16,64,2,128]{3,2,1,0:T(2,128)} %get-tuple-element.266, s32[]{:T(128)S(6)} %copy.112, f32[64,128,128]{2,1,0:T(8,128)} %gather_fusion.2, pred[64]{0:T(512)(128)(4,1)S(1)} %get-tuple-element.237, f32[16,64,2,128]{3,2,1,0:T(2,128)} %get-tuple-element.273), kind=kOutput, calls=%fused_computation.30.clone.1 | convolution fusion | flops 26214400 | bytes 4326464 | tf_op jit(solution)/shard_map/while/body/eval_jaxpr/spq,sfp->sfq/dot_general | solution.py:151
  458.7 6.4 %fusion.134 = f32[16,64,2,128]{3,2,1,0:T(2,128)} fusion(f32[16,64,2,128]{3,2,1,0:T(2,128)} %get-tuple-element.266, s32[]{:T(128)S(6)} %copy.112, f32[64,128,128]{2,1,0:T(8,128)} %gather_fusion.2, pred[64]{0:T(512)(128)(4,1)S(1)} %get-tuple-element.237, f32[16,64,2,128]{3,2,1,0:T(2,128)} %get-tuple-element.273), kind=kOutput, calls=%fused_computation.30.clone.1 | convolution fusion | flops 26214400 | bytes 4326464 | tf_op jit(solution)/shard_map/while/body/eval_jaxpr/spq,sfp->sfq/dot_general | solution.py:151
  468.6 6.4 %fusion.134 = f32[16,64,2,128]{3,2,1,0:T(2,128)} fusion(f32[16,64,2,128]{3,2,1,0:T(2,128)} %get-tuple-element.266, s32[]{:T(128)S(6)} %copy.112, f32[64,128,128]{2,1,0:T(8,128)} %gather_fusion.2, pred[64]{0:T(512)(128)(4,1)S(1)} %get-tuple-element.237, f32[16,64,2,128]{3,2,1,0:T(2,128)} %get-tuple-element.273), kind=kOutput, calls=%fused_computation.30.clone.1 | convolution fusion | flops 26214400 | bytes 4326464 | tf_op jit(solution)/shard_map/while/body/eval_jaxpr/spq,sfp->sfq/dot_general | solution.py:151
  478.5 6.4 %fusion.134 = f32[16,64,2,128]{3,2,1,0:T(2,128)} fusion(f32[16,64,2,128]{3,2,1,0:T(2,128)} %get-tuple-element.266, s32[]{:T(128)S(6)} %copy.112, f32[64,128,128]{2,1,0:T(8,128)} %gather_fusion.2, pred[64]{0:T(512)(128)(4,1)S(1)} %get-tuple-element.237, f32[16,64,2,128]{3,2,1,0:T(2,128)} %get-tuple-element.273), kind=kOutput, calls=%fused_computation.30.clone.1 | convolution fusion | flops 26214400 | bytes 4326464 | tf_op jit(solution)/shard_map/while/body/eval_jaxpr/spq,sfp->sfq/dot_general | solution.py:151
  488.4 6.4 %fusion.134 = f32[16,64,2,128]{3,2,1,0:T(2,128)} fusion(f32[16,64,2,128]{3,2,1,0:T(2,128)} %get-tuple-element.266, s32[]{:T(128)S(6)} %copy.112, f32[64,128,128]{2,1,0:T(8,128)} %gather_fusion.2, pred[64]{0:T(512)(128)(4,1)S(1)} %get-tuple-element.237, f32[16,64,2,128]{3,2,1,0:T(2,128)} %get-tuple-element.273), kind=kOutput, calls=%fused_computation.30.clone.1 | convolution fusion | flops 26214400 | bytes 4326464 | tf_op jit(solution)/shard_map/while/body/eval_jaxpr/spq,sfp->sfq/dot_general | solution.py:151
  498.3 6.4 %fusion.134 = f32[16,64,2,128]{3,2,1,0:T(2,128)} fusion(f32[16,64,2,128]{3,2,1,0:T(2,128)} %get-tuple-element.266, s32[]{:T(128)S(6)} %copy.112, f32[64,128,128]{2,1,0:T(8,128)} %gather_fusion.2, pred[64]{0:T(512)(128)(4,1)S(1)} %get-tuple-element.237, f32[16,64,2,128]{3,2,1,0:T(2,128)} %get-tuple-element.273), kind=kOutput, calls=%fused_computation.30.clone.1 | convolution fusion | flops 26214400 | bytes 4326464 | tf_op jit(solution)/shard_map/while/body/eval_jaxpr/spq,sfp->sfq/dot_general | solution.py:151
  508.2 6.4 %fusion.134 = f32[16,64,2,128]{3,2,1,0:T(2,128)} fusion(f32[16,64,2,128]{3,2,1,0:T(2,128)} %get-tuple-element.266, s32[]{:T(128)S(6)} %copy.112, f32[64,128,128]{2,1,0:T(8,128)} %gather_fusion.2, pred[64]{0:T(512)(128)(4,1)S(1)} %get-tuple-element.237, f32[16,64,2,128]{3,2,1,0:T(2,128)} %get-tuple-element.273), kind=kOutput, calls=%fused_computation.30.clone.1 | convolution fusion | flops 26214400 | bytes 4326464 | tf_op jit(solution)/shard_map/while/body/eval_jaxpr/spq,sfp->sfq/dot_general | solution.py:151
  518.1 6.4 %fusion.134 = f32[16,64,2,128]{3,2,1,0:T(2,128)} fusion(f32[16,64,2,128]{3,2,1,0:T(2,128)} %get-tuple-element.266, s32[]{:T(128)S(6)} %copy.112, f32[64,128,128]{2,1,0:T(8,128)} %gather_fusion.2, pred[64]{0:T(512)(128)(4,1)S(1)} %get-tuple-element.237, f32[16,64,2,128]{3,2,1,0:T(2,128)} %get-tuple-element.273), kind=kOutput, calls=%fused_computation.30.clone.1 | convolution fusion | flops 26214400 | bytes 4326464 | tf_op jit(solution)/shard_map/while/body/eval_jaxpr/spq,sfp->sfq/dot_general | solution.py:151
  528.0 6.4 %fusion.134 = f32[16,64,2,128]{3,2,1,0:T(2,128)} fusion(f32[16,64,2,128]{3,2,1,0:T(2,128)} %get-tuple-element.266, s32[]{:T(128)S(6)} %copy.112, f32[64,128,128]{2,1,0:T(8,128)} %gather_fusion.2, pred[64]{0:T(512)(128)(4,1)S(1)} %get-tuple-element.237, f32[16,64,2,128]{3,2,1,0:T(2,128)} %get-tuple-element.273), kind=kOutput, calls=%fused_computation.30.clone.1 | convolution fusion | flops 26214400 | bytes 4326464 | tf_op jit(solution)/shard_map/while/body/eval_jaxpr/spq,sfp->sfq/dot_general | solution.py:151
  537.9 6.4 %fusion.134 = f32[16,64,2,128]{3,2,1,0:T(2,128)} fusion(f32[16,64,2,128]{3,2,1,0:T(2,128)} %get-tuple-element.266, s32[]{:T(128)S(6)} %copy.112, f32[64,128,128]{2,1,0:T(8,128)} %gather_fusion.2, pred[64]{0:T(512)(128)(4,1)S(1)} %get-tuple-element.237, f32[16,64,2,128]{3,2,1,0:T(2,128)} %get-tuple-element.273), kind=kOutput, calls=%fused_computation.30.clone.1 | convolution fusion | flops 26214400 | bytes 4326464 | tf_op jit(solution)/shard_map/while/body/eval_jaxpr/spq,sfp->sfq/dot_general | solution.py:151
  547.9 6.4 %fusion.134 = f32[16,64,2,128]{3,2,1,0:T(2,128)} fusion(f32[16,64,2,128]{3,2,1,0:T(2,128)} %get-tuple-element.266, s32[]{:T(128)S(6)} %copy.112, f32[64,128,128]{2,1,0:T(8,128)} %gather_fusion.2, pred[64]{0:T(512)(128)(4,1)S(1)} %get-tuple-element.237, f32[16,64,2,128]{3,2,1,0:T(2,128)} %get-tuple-element.273), kind=kOutput, calls=%fused_computation.30.clone.1 | convolution fusion | flops 26214400 | bytes 4326464 | tf_op jit(solution)/shard_map/while/body/eval_jaxpr/spq,sfp->sfq/dot_general | solution.py:151
  554.3 63.8 %scatter_fusion = f32[256,2,128]{2,1,0:T(2,128)S(1)} fusion(f32[256,2,128]{2,1,0:T(2,128)S(1)} %broadcast_in_dim.35, s32[1024]{0:T(1024)S(1)} %copy-done.12, f32[1024,2,128]{2,1,0:T(2,128)} %bitcast.117), kind=kCustom, calls=%fused_computation.3 | custom fusion | flops 262144 | bytes 3149824 | tf_op jit(solution)/shard_map/scatter-add | solution.py:155
  (339 shorter events, 168.3 us)
Async XLA Ops:
  2.0 283.6 %all-to-all-start = ((f32[16,1,64]{2,1,0:T(1,128)}), f32[16,1,64]{2,1,0:T(1,128)S(1)}, u32[]{:S(2)}, u32[]{:S(2)}) async-start(f32[16,1,64]{2,1,0:T(1,128)} %bitcast.22), calls=%async_computation | async-start | bytes 16384 | tf_op jit(solution)/shard_map/all_to_all | solution.py:114
  11.3 288.0 %collective-permute-start.6 = (f32[2,4,1,256]{3,2,0,1:T(1,128)S(1)}, f32[2,4,1,256]{3,2,0,1:T(1,128)S(1)}, u32[]{:S(2)}, u32[]{:S(2)}) collective-permute-start(f32[2,4,1,256]{3,2,0,1:T(1,128)S(1)} %get-tuple-element.145), channel_id=1, source_target_pairs={{0,16},{16,32},{32,48},{48,64},{64,80},{80,96},{96,112},{1,17},{17... | collective-permute-start | bytes 24584 | tf_op jit(solution)/shard_map/ppermute | solution.py:18
  15.3 283.9 %collective-permute-start.7 = (f32[2,4,1,256]{3,2,0,1:T(1,128)S(1)}, f32[2,4,1,256]{3,2,0,1:T(1,128)S(1)}, u32[]{:S(2)}, u32[]{:S(2)}) collective-permute-start(f32[2,4,1,256]{3,2,0,1:T(1,128)S(1)} %get-tuple-element.144), channel_id=1, source_target_pairs={{16,0},{32,16},{48,32},{64,48},{80,64},{96,80},{112,96},{17,1},{33... | collective-permute-start | bytes 24584 | tf_op jit(solution)/shard_map/ppermute | solution.py:19
  18.3 274.8 %collective-permute-start.5 = (f32[4,4,1,256]{3,2,1,0:T(1,128)S(1)}, f32[4,4,1,256]{3,2,1,0:T(1,128)S(1)}, u32[]{:S(2)}, u32[]{:S(2)}) collective-permute-start(f32[4,4,1,256]{3,2,1,0:T(1,128)S(1)} %get-tuple-element.107), channel_id=1, source_target_pairs={{16,0},{32,16},{48,32},{64,48},{80,64},{96,80},{112,96},{17,1},{33... | collective-permute-start | bytes 49160 | tf_op jit(solution)/shard_map/ppermute | solution.py:19
  21.2 241.3 %collective-permute-start.20 = (f32[2,4,16,1]{3,2,0,1:T(8,128)S(1)}, f32[2,4,16,1]{3,2,0,1:T(8,128)S(1)}, u32[]{:S(2)}, u32[]{:S(2)}) collective-permute-start(f32[2,4,16,1]{3,2,0,1:T(8,128)S(1)} %get-tuple-element.127), channel_id=1, source_target_pairs={{1,0},{2,1},{3,2},{4,3},{5,4},{6,5},{7,6},{8,7},{9,8},{10,9},{11,1... | collective-permute-start | bytes 1544 | tf_op jit(solution)/shard_map/ppermute | solution.py:19
  26.2 241.1 %collective-permute-start.21 = (f32[2,4,16,1]{3,2,0,1:T(8,128)S(1)}, f32[2,4,16,1]{3,2,0,1:T(8,128)S(1)}, u32[]{:S(2)}, u32[]{:S(2)}) collective-permute-start(f32[2,4,16,1]{3,2,0,1:T(8,128)S(1)} %get-tuple-element.126), channel_id=1, source_target_pairs={{0,1},{1,2},{2,3},{3,4},{4,5},{5,6},{6,7},{7,8},{8,9},{9,10},{10,1... | collective-permute-start | bytes 1544 | tf_op jit(solution)/shard_map/ppermute | solution.py:18
  31.5 229.7 %copy-start.1 = (f32[2,4,16,256]{3,2,1,0:T(8,128)S(1)}, f32[2,4,16,256]{3,2,1,0:T(8,128)}, u32[]{:S(2)}) copy-start(f32[2,4,16,256]{3,2,1,0:T(8,128)} %param.15) | copy-start | bytes 393220
  31.5 253.1 %copy-start.2 = (f32[2,4,16,256]{3,2,1,0:T(8,128)S(1)}, f32[2,4,16,256]{3,2,1,0:T(8,128)}, u32[]{:S(2)}) copy-start(f32[2,4,16,256]{3,2,1,0:T(8,128)} %param.14) | copy-start | bytes 393220
  261.1 31.9 %copy-start.11 = (s32[16,64]{1,0:T(8,128)}, s32[16,64]{1,0:T(8,128)S(1)}, u32[]{:S(2)}) copy-start(s32[16,64]{1,0:T(8,128)S(1)} %get-tuple-element.319) | copy-start | bytes 12292
  262.5 6.7 %collective-permute-start.1 = (f32[4,4,16,1]{3,2,1,0:T(8,128)S(1)}, f32[4,4,16,1]{3,2,1,0:T(8,128)S(1)}, u32[]{:S(2)}, u32[]{:S(2)}) collective-permute-start(f32[4,4,16,1]{3,2,1,0:T(8,128)S(1)} %get-tuple-element.105), channel_id=1, source_target_pairs={{1,0},{2,1},{3,2},{4,3},{5,4},{6,5},{7,6},{8,7},{9,8},{10,9},{11,1... | collective-permute-start | bytes 3080 | tf_op jit(solution)/shard_map/ppermute | solution.py:19
  267.3 7.6 %collective-permute-start = (f32[4,4,16,1]{3,2,1,0:T(8,128)S(1)}, f32[4,4,16,1]{3,2,1,0:T(8,128)S(1)}, u32[]{:S(2)}, u32[]{:S(2)}) collective-permute-start(f32[4,4,16,1]{3,2,1,0:T(8,128)S(1)} %get-tuple-element.104), channel_id=1, source_target_pairs={{0,1},{1,2},{2,3},{3,4},{4,5},{5,6},{6,7},{7,8},{8,9},{9,10},{10,1... | collective-permute-start | bytes 3080 | tf_op jit(solution)/shard_map/ppermute | solution.py:18
  269.3 6.8 %collective-permute-start.2 = (f32[2,4,16,1]{3,2,0,1:T(8,128)S(1)}, f32[2,4,16,1]{3,2,0,1:T(8,128)S(1)}, u32[]{:S(2)}, u32[]{:S(2)}) collective-permute-start(f32[2,4,16,1]{3,2,0,1:T(8,128)S(1)} %get-tuple-element.143), channel_id=1, source_target_pairs={{0,1},{1,2},{2,3},{3,4},{4,5},{5,6},{6,7},{7,8},{8,9},{9,10},{10,1... | collective-permute-start | bytes 1544 | tf_op jit(solution)/shard_map/ppermute | solution.py:18
  274.9 3.1 collective-permute-start.3
  276.1 14.7 %collective-permute-start.22 = (f32[2,4,1,256]{3,2,0,1:T(1,128)S(1)}, f32[2,4,1,256]{3,2,0,1:T(1,128)S(1)}, u32[]{:S(2)}, u32[]{:S(2)}) collective-permute-start(f32[2,4,1,256]{3,2,0,1:T(1,128)S(1)} %get-tuple-element.129), channel_id=1, source_target_pairs={{16,0},{32,16},{48,32},{64,48},{80,64},{96,80},{112,96},{17,1},{33... | collective-permute-start | bytes 24584 | tf_op jit(solution)/shard_map/ppermute | solution.py:19
  278.1 14.9 %collective-permute-start.23 = (f32[2,4,1,256]{3,2,0,1:T(1,128)S(1)}, f32[2,4,1,256]{3,2,0,1:T(1,128)S(1)}, u32[]{:S(2)}, u32[]{:S(2)}) collective-permute-start(f32[2,4,1,256]{3,2,0,1:T(1,128)S(1)} %get-tuple-element.128), channel_id=1, source_target_pairs={{0,16},{16,32},{32,48},{48,64},{64,80},{80,96},{96,112},{1,17},{17... | collective-permute-start | bytes 24584 | tf_op jit(solution)/shard_map/ppermute | solution.py:18
  285.5 37.5 %copy-start.7 = (f32[4,16,256]{2,1,0:T(8,128)}, f32[4,16,256]{2,1,0:T(8,128)S(1)}, u32[]{:S(2)}) copy-start(f32[4,16,256]{2,1,0:T(8,128)S(1)} %slice.610) | copy-start | bytes 196612
  285.5 37.4 %copy-start.8 = (f32[4,16,256]{2,1,0:T(8,128)}, f32[4,16,256]{2,1,0:T(8,128)S(1)}, u32[]{:S(2)}) copy-start(f32[4,16,256]{2,1,0:T(8,128)S(1)} %slice.606) | copy-start | bytes 196612
  285.6 35.6 %all-to-all-start.1 = ((f32[16,64,256]{2,1,0:T(8,128)}), f32[16,64,256]{2,1,0:T(8,128)S(1)}, u32[]{:S(2)}, u32[]{:S(2)}) async-start(f32[16,64,256]{2,1,0:T(8,128)} %get-tuple-element.63), calls=%async_computation.1 | async-start | bytes 2097152 | tf_op jit(solution)/shard_map/all_to_all | solution.py:113
  290.8 3.1 collective-permute-start.4
  294.0 71.6 %copy-start.3 = (f32[4,17,256]{2,1,0:T(8,128)}, f32[4,17,256]{2,1,0:T(8,128)S(1)}, u32[]{:S(2)}) copy-start(f32[4,17,256]{2,1,0:T(8,128)S(1)} %get-tuple-element.110) | copy-start | bytes 208900
  294.0 81.6 %copy-start.5 = (f32[4,17,256]{2,1,0:T(8,128)}, f32[4,17,256]{2,1,0:T(8,128)S(1)}, u32[]{:S(2)}) copy-start(f32[4,17,256]{2,1,0:T(8,128)S(1)} %get-tuple-element.111) | copy-start | bytes 208900
  294.0 28.9 %copy-start.9 = (f32[4,16,256]{2,1,0:T(8,128)}, f32[4,16,256]{2,1,0:T(8,128)S(1)}, u32[]{:S(2)}) copy-start(f32[4,16,256]{2,1,0:T(8,128)S(1)} %slice.616) | copy-start | bytes 196612
  294.1 28.9 %copy-start.10 = (f32[4,16,256]{2,1,0:T(8,128)}, f32[4,16,256]{2,1,0:T(8,128)S(1)}, u32[]{:S(2)}) copy-start(f32[4,16,256]{2,1,0:T(8,128)S(1)} %slice.612) | copy-start | bytes 196612
  294.3 12.2 %collective-permute-start.24 = (f32[2,4,16,1]{3,2,0,1:T(8,128)S(1)}, f32[2,4,16,1]{3,2,0,1:T(8,128)S(1)}, u32[]{:S(2)}, u32[]{:S(2)}) collective-permute-start(f32[2,4,16,1]{3,2,0,1:T(8,128)S(1)} %get-tuple-element.123), channel_id=1, source_target_pairs={{1,0},{2,1},{3,2},{4,3},{5,4},{6,5},{7,6},{8,7},{9,8},{10,9},{11,1... | collective-permute-start | bytes 1544 | tf_op jit(solution)/shard_map/ppermute | solution.py:19
  299.3 7.2 %collective-permute-start.25 = (f32[2,4,16,1]{3,2,0,1:T(8,128)S(1)}, f32[2,4,16,1]{3,2,0,1:T(8,128)S(1)}, u32[]{:S(2)}, u32[]{:S(2)}) collective-permute-start(f32[2,4,16,1]{3,2,0,1:T(8,128)S(1)} %get-tuple-element.122), channel_id=1, source_target_pairs={{0,1},{1,2},{2,3},{3,4},{4,5},{5,6},{6,7},{7,8},{8,9},{9,10},{10,1... | collective-permute-start | bytes 1544 | tf_op jit(solution)/shard_map/ppermute | solution.py:18
  300.0 6.6 %collective-permute-start.26 = (f32[2,4,1,256]{3,2,0,1:T(1,128)S(1)}, f32[2,4,1,256]{3,2,0,1:T(1,128)S(1)}, u32[]{:S(2)}, u32[]{:S(2)}) collective-permute-start(f32[2,4,1,256]{3,2,0,1:T(1,128)S(1)} %get-tuple-element.125), channel_id=1, source_target_pairs={{16,0},{32,16},{48,32},{64,48},{80,64},{96,80},{112,96},{17,1},{33... | collective-permute-start | bytes 24584 | tf_op jit(solution)/shard_map/ppermute | solution.py:19
  302.1 5.1 collective-permute-start.27
  307.4 12.2 %collective-permute-start.28 = (f32[2,4,16,1]{3,2,0,1:T(8,128)S(1)}, f32[2,4,16,1]{3,2,0,1:T(8,128)S(1)}, u32[]{:S(2)}, u32[]{:S(2)}) collective-permute-start(f32[2,4,16,1]{3,2,0,1:T(8,128)S(1)} %get-tuple-element.119), channel_id=1, source_target_pairs={{1,0},{2,1},{3,2},{4,3},{5,4},{6,5},{7,6},{8,7},{9,8},{10,9},{11,1... | collective-permute-start | bytes 1544 | tf_op jit(solution)/shard_map/ppermute | solution.py:19
  312.5 7.1 %collective-permute-start.29 = (f32[2,4,16,1]{3,2,0,1:T(8,128)S(1)}, f32[2,4,16,1]{3,2,0,1:T(8,128)S(1)}, u32[]{:S(2)}, u32[]{:S(2)}) collective-permute-start(f32[2,4,16,1]{3,2,0,1:T(8,128)S(1)} %get-tuple-element.118), channel_id=1, source_target_pairs={{0,1},{1,2},{2,3},{3,4},{4,5},{5,6},{6,7},{7,8},{8,9},{9,10},{10,1... | collective-permute-start | bytes 1544 | tf_op jit(solution)/shard_map/ppermute | solution.py:18
  313.3 6.6 %collective-permute-start.30 = (f32[2,4,1,256]{3,2,0,1:T(1,128)S(1)}, f32[2,4,1,256]{3,2,0,1:T(1,128)S(1)}, u32[]{:S(2)}, u32[]{:S(2)}) collective-permute-start(f32[2,4,1,256]{3,2,0,1:T(1,128)S(1)} %get-tuple-element.121), channel_id=1, source_target_pairs={{16,0},{32,16},{48,32},{64,48},{80,64},{96,80},{112,96},{17,1},{33... | collective-permute-start | bytes 24584 | tf_op jit(solution)/shard_map/ppermute | solution.py:19
  315.2 5.3 collective-permute-start.31
  325.4 40.1 %collective-permute-start.10 = (f32[2,4,1,256]{3,2,0,1:T(1,128)S(1)}, f32[2,4,1,256]{3,2,0,1:T(1,128)S(1)}, u32[]{:S(2)}, u32[]{:S(2)}) collective-permute-start(f32[2,4,1,256]{3,2,0,1:T(1,128)S(1)} %get-tuple-element.141), channel_id=1, source_target_pairs={{0,16},{16,32},{32,48},{48,64},{64,80},{80,96},{96,112},{1,17},{17... | collective-permute-start | bytes 24584 | tf_op jit(solution)/shard_map/ppermute | solution.py:18
  329.7 35.8 %collective-permute-start.11 = (f32[2,4,1,256]{3,2,0,1:T(1,128)S(1)}, f32[2,4,1,256]{3,2,0,1:T(1,128)S(1)}, u32[]{:S(2)}, u32[]{:S(2)}) collective-permute-start(f32[2,4,1,256]{3,2,0,1:T(1,128)S(1)} %get-tuple-element.140), channel_id=1, source_target_pairs={{16,0},{32,16},{48,32},{64,48},{80,64},{96,80},{112,96},{17,1},{33... | collective-permute-start | bytes 24584 | tf_op jit(solution)/shard_map/ppermute | solution.py:19
  331.7 14.0 %collective-permute-start.8 = (f32[2,4,16,1]{3,2,0,1:T(8,128)S(1)}, f32[2,4,16,1]{3,2,0,1:T(8,128)S(1)}, u32[]{:S(2)}, u32[]{:S(2)}) collective-permute-start(f32[2,4,16,1]{3,2,0,1:T(8,128)S(1)} %get-tuple-element.139), channel_id=1, source_target_pairs={{0,1},{1,2},{2,3},{3,4},{4,5},{5,6},{6,7},{7,8},{8,9},{9,10},{10,1... | collective-permute-start | bytes 1544 | tf_op jit(solution)/shard_map/ppermute | solution.py:18
  331.8 18.7 %collective-permute-start.9 = (f32[2,4,16,1]{3,2,0,1:T(8,128)S(1)}, f32[2,4,16,1]{3,2,0,1:T(8,128)S(1)}, u32[]{:S(2)}, u32[]{:S(2)}) collective-permute-start(f32[2,4,16,1]{3,2,0,1:T(8,128)S(1)} %get-tuple-element.138), channel_id=1, source_target_pairs={{1,0},{2,1},{3,2},{4,3},{5,4},{6,5},{7,6},{8,7},{9,8},{10,9},{11,1... | collective-permute-start | bytes 1544 | tf_op jit(solution)/shard_map/ppermute | solution.py:19
  337.0 35.2 %collective-permute-start.34 = (f32[2,4,1,256]{3,2,0,1:T(1,128)S(1)}, f32[2,4,1,256]{3,2,0,1:T(1,128)S(1)}, u32[]{:S(2)}, u32[]{:S(2)}) collective-permute-start(f32[2,4,1,256]{3,2,0,1:T(1,128)S(1)} %get-tuple-element.117), channel_id=1, source_target_pairs={{16,0},{32,16},{48,32},{64,48},{80,64},{96,80},{112,96},{17,1},{33... | collective-permute-start | bytes 24584 | tf_op jit(solution)/shard_map/ppermute | solution.py:19
  342.0 52.2 %all-to-all-start.2 = ((f32[16,64,256]{2,1,0:T(8,128)}), f32[16,64,256]{2,1,0:T(8,128)S(1)}, u32[]{:S(2)}, u32[]{:S(2)}) async-start(f32[16,64,256]{2,1,0:T(8,128)} %fusion.27), calls=%async_computation.2 | async-start | bytes 2097152 | tf_op jit(solution)/shard_map/all_to_all | solution.py:144
  345.7 13.1 %collective-permute-start.32 = (f32[2,4,16,1]{3,2,0,1:T(8,128)S(1)}, f32[2,4,16,1]{3,2,0,1:T(8,128)S(1)}, u32[]{:S(2)}, u32[]{:S(2)}) collective-permute-start(f32[2,4,16,1]{3,2,0,1:T(8,128)S(1)} %get-tuple-element.115), channel_id=1, source_target_pairs={{1,0},{2,1},{3,2},{4,3},{5,4},{6,5},{7,6},{8,7},{9,8},{10,9},{11,1... | collective-permute-start | bytes 1544 | tf_op jit(solution)/shard_map/ppermute | solution.py:19
  350.4 15.0 %collective-permute-start.33 = (f32[2,4,16,1]{3,2,0,1:T(8,128)S(1)}, f32[2,4,16,1]{3,2,0,1:T(8,128)S(1)}, u32[]{:S(2)}, u32[]{:S(2)}) collective-permute-start(f32[2,4,16,1]{3,2,0,1:T(8,128)S(1)} %get-tuple-element.114), channel_id=1, source_target_pairs={{0,1},{1,2},{2,3},{3,4},{4,5},{5,6},{6,7},{7,8},{8,9},{9,10},{10,1... | collective-permute-start | bytes 1544 | tf_op jit(solution)/shard_map/ppermute | solution.py:18
  358.8 16.8 %collective-permute-start.35 = (f32[2,4,1,256]{3,2,0,1:T(1,128)S(1)}, f32[2,4,1,256]{3,2,0,1:T(1,128)S(1)}, u32[]{:S(2)}, u32[]{:S(2)}) collective-permute-start(f32[2,4,1,256]{3,2,0,1:T(1,128)S(1)} %get-tuple-element.116), channel_id=1, source_target_pairs={{0,16},{16,32},{32,48},{48,64},{64,80},{80,96},{96,112},{1,17},{17... | collective-permute-start | bytes 24584 | tf_op jit(solution)/shard_map/ppermute | solution.py:18
  365.7 27.7 %copy-start.4 = (f32[4,17,256]{2,1,0:T(8,128)S(1)}, f32[4,17,256]{2,1,0:T(8,128)}, u32[]{:S(2)}) copy-start(f32[4,17,256]{2,1,0:T(8,128)} %copy-done.3) | copy-start | bytes 208900
  365.9 11.8 %collective-permute-start.14 = (f32[2,4,1,256]{3,2,0,1:T(1,128)S(1)}, f32[2,4,1,256]{3,2,0,1:T(1,128)S(1)}, u32[]{:S(2)}, u32[]{:S(2)}) collective-permute-start(f32[2,4,1,256]{3,2,0,1:T(1,128)S(1)} %get-tuple-element.137), channel_id=1, source_target_pairs={{0,16},{16,32},{32,48},{48,64},{64,80},{80,96},{96,112},{1,17},{17... | collective-permute-start | bytes 24584 | tf_op jit(solution)/shard_map/ppermute | solution.py:18
  368.2 9.6 %collective-permute-start.15 = (f32[2,4,1,256]{3,2,0,1:T(1,128)S(1)}, f32[2,4,1,256]{3,2,0,1:T(1,128)S(1)}, u32[]{:S(2)}, u32[]{:S(2)}) collective-permute-start(f32[2,4,1,256]{3,2,0,1:T(1,128)S(1)} %get-tuple-element.136), channel_id=1, source_target_pairs={{16,0},{32,16},{48,32},{64,48},{80,64},{96,80},{112,96},{17,1},{33... | collective-permute-start | bytes 24584 | tf_op jit(solution)/shard_map/ppermute | solution.py:19
  370.2 7.4 %collective-permute-start.12 = (f32[2,4,16,1]{3,2,0,1:T(8,128)S(1)}, f32[2,4,16,1]{3,2,0,1:T(8,128)S(1)}, u32[]{:S(2)}, u32[]{:S(2)}) collective-permute-start(f32[2,4,16,1]{3,2,0,1:T(8,128)S(1)} %get-tuple-element.135), channel_id=1, source_target_pairs={{0,1},{1,2},{2,3},{3,4},{4,5},{5,6},{6,7},{7,8},{8,9},{9,10},{10,1... | collective-permute-start | bytes 1544 | tf_op jit(solution)/shard_map/ppermute | solution.py:18
  372.1 5.5 collective-permute-start.13
  375.6 17.7 %copy-start.6 = (f32[4,17,256]{2,1,0:T(8,128)S(1)}, f32[4,17,256]{2,1,0:T(8,128)}, u32[]{:S(2)}) copy-start(f32[4,17,256]{2,1,0:T(8,128)} %copy-done.5) | copy-start | bytes 208900
  375.6 20.1 %copy-start = (f32[32,128,128]{2,1,0:T(8,128)S(1)}, f32[32,128,128]{2,1,0:T(8,128)}, u32[]{:S(2)}) copy-start(f32[32,128,128]{2,1,0:T(8,128)} %get-tuple-element.277) | copy-start | bytes 6291460
  379.0 11.3 %collective-permute-start.16 = (f32[2,4,16,1]{3,2,0,1:T(8,128)S(1)}, f32[2,4,16,1]{3,2,0,1:T(8,128)S(1)}, u32[]{:S(2)}, u32[]{:S(2)}) collective-permute-start(f32[2,4,16,1]{3,2,0,1:T(8,128)S(1)} %get-tuple-element.131), channel_id=1, source_target_pairs={{0,1},{1,2},{2,3},{3,4},{4,5},{5,6},{6,7},{7,8},{8,9},{9,10},{10,1... | collective-permute-start | bytes 1544 | tf_op jit(solution)/shard_map/ppermute | solution.py:18
  379.0 11.3 %collective-permute-start.17 = (f32[2,4,16,1]{3,2,0,1:T(8,128)S(1)}, f32[2,4,16,1]{3,2,0,1:T(8,128)S(1)}, u32[]{:S(2)}, u32[]{:S(2)}) collective-permute-start(f32[2,4,16,1]{3,2,0,1:T(8,128)S(1)} %get-tuple-element.130), channel_id=1, source_target_pairs={{1,0},{2,1},{3,2},{4,3},{5,4},{6,5},{7,6},{8,7},{9,8},{10,9},{11,1... | collective-permute-start | bytes 1544 | tf_op jit(solution)/shard_map/ppermute | solution.py:19
  384.2 6.3 %collective-permute-start.18 = (f32[2,4,1,256]{3,2,0,1:T(1,128)S(1)}, f32[2,4,1,256]{3,2,0,1:T(1,128)S(1)}, u32[]{:S(2)}, u32[]{:S(2)}) collective-permute-start(f32[2,4,1,256]{3,2,0,1:T(1,128)S(1)} %get-tuple-element.133), channel_id=1, source_target_pairs={{0,16},{16,32},{32,48},{48,64},{64,80},{80,96},{96,112},{1,17},{17... | collective-permute-start | bytes 24584 | tf_op jit(solution)/shard_map/ppermute | solution.py:18
  388.4 5.0 collective-permute-start.19
  395.7 158.6 %copy-start.12 = (s32[1024]{0:T(1024)S(1)}, s32[1024]{0:T(1024)}, u32[]{:S(2)}) copy-start(s32[1024]{0:T(1024)} %reshape.191) | copy-start | bytes 12292
where the time goes:
time: 626 us; the launch traced here: 619 us
  matrix products  242 us (39%)
  local copies, waits for them, and re-layouts  148 us (24%)
  starting transfers between devices  114 us (18%)
  other arithmetic  90.8 us (15%)
  waiting for transfers between devices  21.6 us (3%)
    dot_general x16, matrix products, weigh_slots(): jnp.einsum('spq,fsq->sfp', block_picks, atm_picks, precision=highest)  137 us
    dot_general x16, matrix products, unweigh_slots(): return jnp.einsum('spq,sfp->sfq', block_picks, slot_rows, precision=highest)  103 us
    gather x16, local copies, waits for them, and re-layouts, weigh_slots(): block_picks = jnp.take(weights, block_ids, axis=0)  70.3 us
    scatter-add x1, other arithmetic, on_device(): jax.ops.segment_sum(unweighed.reshape(-1, 2, BLOCK), slot_lists[1].reshap...  63.8 us
    ppermute x18, starting transfers between devices, padded(): after = lax.ppermute(first, axis, down)  55.9 us
    gather x16, local copies, waits for them, and re-layouts, unweigh_slots(): block_picks = jnp.take(weights, block_ids, axis=0)  44.8 us
    ppermute x18, starting transfers between devices, padded(): before = lax.ppermute(last, axis, up)  41.1 us
    ppermute x18, waiting for transfers between devices, padded(): after = lax.ppermute(first, axis, down)  13 us
  transfers between devices with their start and end apart: 39, of which 8 were waited for; matrix products, arithmetic and copies ran while one was open for 41% of the time, Pallas kernels for 0%

commit v1 on v0

v1 whole, which is shorter than its diff:
```python
import jax
import jax.numpy as jnp
from jax import lax
from jax.experimental import pallas as pl
from jax.experimental.pallas import tpu as pltpu
from jax.sharding import PartitionSpec as P

MESH = pl.DeviceIdType.MESH
F32 = jnp.float32
BF16 = jnp.bfloat16
BLOCK = 128
CAP = 64
STEPS = 4
LEV = 4
ROWS = 16
COLS = 256
XROWS = 24
XCOLS = 384
TRC, COT, DIF, VEL, MSK = 0, 8, 16, 28, 36
PLANES = 40
HALF = PLANES // 2
EA, EB, NA, NB, BK = 0, 4, 8, 12, 16
WB = 32
ATM = 256
OCN = 32
MSG = 2 * OCN
BATCH = 4


def iota(shape, axis):
    return lax.broadcasted_iota(jnp.int32, shape, axis)


def split(x):
    hi = x.astype(BF16)
    return hi, (x - hi.astype(F32)).astype(BF16)


def dot(a, b):
    return lax.dot_general(a, b, (((1,), (0,)), ((), ())), preferred_element_type=F32)


def dot_t(a, b):
    return lax.dot_general(a, b, (((1,), (1,)), ((), ())), preferred_element_type=F32)


def east(x):
    return pltpu.roll(x, XCOLS - 1, 1)


def west(x):
    return pltpu.roll(x, 1, 1)


def north(x):
    return pltpu.roll(x, XROWS - 1, 0)


def south(x):
    return pltpu.roll(x, 1, 0)


def kernel(
    n_lat, n_lon,
    tracers, cotangent, land, diffusion, velocity, weights, atm, slots_s, slots_v,
    out_t, out_c, out_g,
    ext, mask_i, atm_v, weights_v, coef, force, ssum,
    send_n, send_s, send_c, recv_n, recv_s, recv_e, recv_w, recv_d,
    fsend_r, fsend_c, frecv_n, frecv_s, frecv_e, frecv_w, frecv_d,
    w_fwd, w_rev, x_rows, x_cat, table_f, picked, p_send, p_recv,
    s_all, v_cat, table_r, z_rows, z_cat, ids, hot,
    load_sem, halo_send, halo_recv, p_ssem, p_rsem, s_ssem, s_rsem, f_send, f_recv, out_sem,
):
    lat, lon = lax.axis_index("lat"), lax.axis_index("lon")
    up, down = lax.rem(lat + 1, n_lat), lax.rem(lat + n_lat - 1, n_lat)
    right, left = lax.rem(lon + 1, n_lon), lax.rem(lon + n_lon - 1, n_lon)
    loads = [
        (tracers, ext.at[TRC : TRC + 8, 0:ROWS, 0:COLS]),
        (cotangent, ext.at[COT : COT + 8, 0:ROWS, 0:COLS]),
        (diffusion, ext.at[DIF : DIF + 12, 0:ROWS, 0:COLS]),
        (velocity, ext.at[VEL : VEL + 8, 0:ROWS, 0:COLS]),
        (land, mask_i),
        (atm, atm_v),
        (weights, weights_v),
    ]
    loads = [pltpu.make_async_copy(a, b, load_sem.at[i]) for i, (a, b) in enumerate(loads)]
    for copy in loads:
        copy.start()

    barrier = pltpu.get_barrier_semaphore()
    peers = [(up, lon), (down, lon), (up, left), (up, right), (down, left), (down, right)]
    for peer in peers:
        pl.semaphore_signal(barrier, inc=1, device_id=peer, device_id_type=MESH)

    @pl.loop(1, n_lon)
    def _(step):
        pl.semaphore_signal(barrier, inc=1, device_id=(lat, lax.rem(lon + step, n_lon)), device_id_type=MESH)

    pl.semaphore_wait(barrier, len(peers) + n_lon - 1)

    lane = iota((8, 128), 1)
    row = iota((8, 128), 0)
    row2 = iota((8, COLS), 0)
    low = row2 < 4
    group = lax.rem((lane + 4) // 8, 16)
    for copy in loads[:5]:
        copy.wait()
    ext[MSK : MSK + 4, 0:ROWS, 0:COLS] = mask_i[...].astype(F32)

    @pl.loop(0, HALF)
    def _(p):
        first, last = ext[p, 0:8, 0:COLS], ext[p, 8:16, 0:COLS]
        first2, last2 = ext[p + HALF, 0:8, 0:COLS], ext[p + HALF, 8:16, 0:COLS]
        send_n[p] = jnp.where(low, pltpu.roll(last2, 4, 0), last)
        send_s[p] = jnp.where(low, first, pltpu.roll(first2, 4, 0))

    def remote(src, dst, sems, i, peer):
        return pltpu.make_async_remote_copy(
            src_ref=src, dst_ref=dst, send_sem=sems[0].at[i], recv_sem=sems[1].at[i], device_id=peer, device_id_type=MESH
        )

    halo = (halo_send, halo_recv)
    halos = [remote(send_n, recv_s, halo, 0, (up, lon)), remote(send_s, recv_n, halo, 1, (down, lon))]
    for copy in halos:
        copy.start()

    def pack_columns(plane_of, count, put):
        for tile in range(-(-count // 16)):
            for r in (0, 8):
                acc = jnp.zeros((8, 128), F32)
                for q in range(min(16, count - 16 * tile)):
                    p = plane_of(16 * tile + q)
                    edge = jnp.where(lane < 4, p(r, 0), p(r, 128))
                    if q:
                        edge = pltpu.roll(edge, 8 * q, 1)
                    acc = jnp.where(group == q, edge, acc)
                put(r, tile, acc)

    def put_c(r, tile, value):
        send_c[r : r + 8, 128 * tile : 128 * tile + 128] = value

    pack_columns(lambda p: lambda r, c: ext[p, r : r + 8, c : c + 128], PLANES, put_c)

    def column_copies(src, to_e, to_w, to_d, sems, base):
        first, last = src.at[0:8], src.at[8:16]
        return [
            remote(src, to_w, sems, base, (lat, right)),
            remote(src, to_e, sems, base + 1, (lat, left)),
            remote(last, to_d.at[3], sems, base + 2, (up, right)),
            remote(last, to_d.at[1], sems, base + 3, (up, left)),
            remote(first, to_d.at[2], sems, base + 4, (down, right)),
            remote(first, to_d.at[0], sems, base + 5, (down, left)),
        ]

    columns = column_copies(send_c, recv_e, recv_w, recv_d, halo, 2)
    for copy in columns:
        copy.start()
    halos += columns

    for copy in loads[5:]:
        copy.wait()

    @pl.loop(0, WB // 2)
    def _(pair):
        for i in range(2):
            hi, lo = split(weights_v[2 * pair + i])
            w_fwd[pair, 128 * i : 128 * i + 128, 0:128] = hi
            w_fwd[pair, 128 * i : 128 * i + 128, 128:256] = lo
            w_rev[pair, 0:128, 128 * i : 128 * i + 128] = hi
            w_rev[pair, 128:256, 128 * i : 128 * i + 128] = lo

    for f in range(2):
        x_rows[pl.ds(f, ATM, stride=2), :] = atm_v[f]
    hi, lo = split(x_rows[...])
    x_cat[0 : 2 * ATM, 0:128] = hi
    x_cat[0 : 2 * ATM, 128:256] = hi
    x_cat[2 * ATM :, 0:128] = lo
    x_cat[2 * ATM :, 128:256] = lo

    @pl.loop(0, WB // 2)
    def _(pair):
        both = w_fwd[pair]
        out = dot_t(x_cat[0 : 2 * ATM], both) + dot_t(x_cat[2 * ATM :], both)
        at = pl.multiple_of(pair * (4 * ATM), 4 * ATM)
        table_f[pl.ds(at, 2 * ATM), :] = out[:, 0:128]
        table_f[pl.ds(at + 2 * ATM, 2 * ATM), :] = out[:, 128:256]

    for copy in halos:
        copy.wait_recv()

    edge_row = jnp.where(row < 4, (lat < n_lat - 1).astype(F32), (lat > 0).astype(F32))
    edge_row2 = jnp.where(low, (lat < n_lat - 1).astype(F32), (lat > 0).astype(F32))

    @pl.loop(0, HALF)
    def _(p):
        from_n, from_s = recv_n[p], recv_s[p]
        ext[p, 16:24, 0:COLS] = jnp.where(low, from_n, from_s)
        ext[p + HALF, 16:24, 0:COLS] = pltpu.roll(jnp.where(low, from_s, from_n), 4, 0)

    for p in range(MSK, MSK + 4):
        ext[p, 16:24, 0:COLS] = ext[p, 16:24, 0:COLS] * edge_row2

    from_east = lax.rem(lane, 8) < 4
    keep = jnp.logical_or(lane < 4, lane >= 124)

    def unpack_columns(from_e, from_w, from_d, count, put):
        for tile in range(-(-count // 16)):
            t = slice(128 * tile, 128 * tile + 128)
            for r in (0, 8, 16):
                if r < 16:
                    e, w = from_e[r : r + 8, t], from_w[r : r + 8, t]
                else:
                    e = jnp.where(row < 4, from_d[0, :, t], from_d[1, :, t])
                    w = jnp.where(row < 4, from_d[2, :, t], from_d[3, :, t])
                both = jnp.where(from_east, e, w)
                for q in range(min(16, count - 16 * tile)):
                    value = pltpu.roll(both, 128 - 8 * q, 1) if q else both
                    put(16 * tile + q, r, jnp.where(keep, value, 0.0))

    def put_x(p, r, value):
        if p >= MSK and r == 16:
            value = value * edge_row
        ext[p, r : r + 8, 256:384] = value

    unpack_columns(recv_e, recv_w, recv_d, PLANES, put_x)

    for lev in range(LEV):
        m = ext[MSK + lev]
        me, mn = m * east(m), m * north(m)
        k, v = ext[DIF + lev] * me, ext[VEL + lev] * me
        coef[EA + lev] = jnp.maximum(v, 0.0) + k
        coef[EB + lev] = jnp.minimum(v, 0.0) - k
        k, v = ext[DIF + LEV + lev] * mn, ext[VEL + LEV + lev] * mn
        coef[NA + lev] = jnp.maximum(v, 0.0) + k
        coef[NB + lev] = jnp.minimum(v, 0.0) - k
        if lev < LEV - 1:
            coef[BK + lev] = ext[DIF + 2 * LEV + lev] * m * ext[MSK + lev + 1]

    def retreat():
        for f in range(2):
            above = None
            for lev in range(LEV):
                p = COT + LEV * f + lev
                v = ext[p]
                step_x, step_y = east(v) - v, north(v) - v
                new = v + (coef[EA + lev] * step_x + west(coef[EB + lev] * step_x))
                new = new + (coef[NA + lev] * step_y + south(coef[NB + lev] * step_y))
                if lev < LEV - 1:
                    vertical = coef[BK + lev] * (ext[p + 1] - v)
                    new = new + vertical
                if above is not None:
                    new = new - above
                above = vertical
                ext[p] = new

    def advance():
        for f in range(2):
            above = None
            for lev in range(LEV):
                p = TRC + LEV * f + lev
                v = ext[p]
                flux_x = coef[EA + lev] * v + coef[EB + lev] * east(v)
                flux_y = coef[NA + lev] * v + coef[NB + lev] * north(v)
                new = v - (flux_x - west(flux_x)) - (flux_y - south(flux_y))
                if lev < LEV - 1:
                    below = coef[BK + lev] * (v - ext[p + 1])
                    new = new - below
                if above is not None:
                    new = new + above
                above = below
                if lev == 0:
                    new = new + force[f]
                ext[p] = new

    for f in range(2):
        ssum[f] = ext[COT + LEV * f, 0:ROWS, 0:COLS]

    @pl.loop(0, STEPS - 1)
    def _(step):
        retreat()
        for f in range(2):
            ssum[f] = ssum[f] + ext[COT + LEV * f, 0:ROWS, 0:COLS]

    mask0 = ext[MSK, 0:ROWS, 0:COLS]
    for f in range(2):
        surface = ssum[f] * mask0
        for h in range(2):
            s_all[lon, pl.ds(2 * h + f, ROWS, stride=4), :] = surface[:, 128 * h : 128 * h + 128]

    def surface_copy(step):
        return pltpu.make_async_remote_copy(
            src_ref=s_all.at[lon], dst_ref=s_all.at[lon], send_sem=s_ssem.at[step], recv_sem=s_rsem.at[step],
            device_id=(lat, lax.rem(lon + step, n_lon)), device_id_type=MESH,
        )

    @pl.loop(1, n_lon)
    def _(step):
        surface_copy(step).start()

    def partial(step):
        k = lax.rem(lon + step, n_lon)
        for s in range(CAP):
            at = slots_s[2, k, s] * (2 * ATM) + 2 * slots_s[1, k, s]
            picked[2 * s : 2 * s + 2, :] = table_f[pl.ds(at, 2), :]
        onehot = (slots_v[0, pl.ds(k, 1), :] == iota((OCN, CAP), 0)).astype(BF16)
        for f in range(2):
            hi, lo = split(picked[pl.ds(f, CAP, stride=2), :])
            p_send[step, pl.ds(f, OCN, stride=2), :] = dot(onehot, hi) + dot(onehot, lo)

    def partial_copy(step):
        return pltpu.make_async_remote_copy(
            src_ref=p_send.at[step], dst_ref=p_recv.at[step], send_sem=p_ssem.at[step], recv_sem=p_rsem.at[step],
            device_id=(lat, lax.rem(lon + step, n_lon)), device_id_type=MESH,
        )

    @pl.loop(1, n_lon)
    def _(step):
        partial(step)
        partial_copy(step).start()

    partial(0)
    retreat()
    adjoint_out = pltpu.make_async_copy(ext.at[COT : COT + 8, 0:ROWS, 0:COLS], out_c, out_sem.at[0])
    adjoint_out.start()

    def reverse(batch):
        for i in range(BATCH):
            step = batch * BATCH + i
            k = lax.rem(lon + n_lon - step, n_lon)
            hi, lo = split(s_all[k])
            v_cat[MSG * i : MSG * i + MSG, 0:128] = hi
            v_cat[MSG * i : MSG * i + MSG, 128:256] = hi
            v_cat[MSG * (BATCH + i) : MSG * (BATCH + i + 1), 0:128] = lo
            v_cat[MSG * (BATCH + i) : MSG * (BATCH + i + 1), 128:256] = lo
        size = MSG * BATCH

        @pl.loop(0, WB // 2)
        def _(pair):
            both = w_rev[pair]
            out = dot(v_cat[0:size], both) + dot(v_cat[size:], both)
            at = pl.multiple_of(pair * (2 * size), 2 * size)
            table_r[pl.ds(at, size), :] = out[:, 0:128]
            table_r[pl.ds(at + size, size), :] = out[:, 128:256]

        @pl.loop(0, BATCH)
        def _(i):
            k = lax.rem(lon + n_lon - (batch * BATCH + i), n_lon)
            base = pl.multiple_of(k * (2 * CAP), 2 * CAP)
            for s in range(CAP):
                at = slots_s[2, k, s] * size + i * MSG + 2 * jnp.maximum(slots_s[0, k, s], 0)
                z_rows[pl.ds(base + 2 * s, 2), :] = table_r[pl.ds(at, 2), :]

    def wait_surface(batch):
        for step in range(batch * BATCH, batch * BATCH + BATCH):
            if step:
                surface_copy(step).wait_recv()

    wait_surface(0)
    reverse(0)

    total = p_send[0]
    for step in range(1, 16):
        partial_copy(step).wait_recv()
        total = total + p_recv[step]
    p_send[0] = total
    for f in range(2):
        for h in range(2):
            part = p_send[0, pl.ds(2 * h + f, ROWS, stride=4), :]
            force[f, 0:ROWS, 128 * h : 128 * h + 128] = part * mask0[:, 128 * h : 128 * h + 128]
        fsend_r[f] = force[f, 0:ROWS, 0:COLS]

    fsem = (f_send, f_recv)

    def put_f(r, tile, value):
        fsend_c[r : r + 8, :] = value

    pack_columns(lambda p: lambda r, c: force[p, r : r + 8, c : c + 128], 2, put_f)
    fcopies = [
        remote(fsend_r.at[:, 8:16], frecv_s, fsem, 0, (up, lon)),
        remote(fsend_r.at[:, 0:8], frecv_n, fsem, 1, (down, lon)),
    ] + column_copies(fsend_c, frecv_e, frecv_w, frecv_d, fsem, 2)
    for copy in fcopies:
        copy.start()

    wait_surface(1)
    reverse(1)

    for copy in fcopies:
        copy.wait_recv()
    for f in range(2):
        force[f, 16:24, 0:COLS] = jnp.where(low, frecv_n[f], frecv_s[f]) * edge_row2

    def put_force(p, r, value):
        force[p, r : r + 8, 256:384] = value * edge_row if r == 16 else value

    unpack_columns(frecv_e, frecv_w, frecv_d, 2, put_force)

    @pl.loop(0, STEPS)
    def _(step):
        advance()

    tracer_out = pltpu.make_async_copy(ext.at[TRC : TRC + 8, 0:ROWS, 0:COLS], out_t, out_sem.at[1])
    tracer_out.start()

    for batch in range(2, 16 // BATCH):
        wait_surface(batch)
        reverse(batch)

    ids[:, 0:CAP] = jnp.where(slots_v[0] >= 0, slots_v[1], -1)
    for g in range(8):
        pick = jnp.concatenate([ids[2 * g : 2 * g + 1, 0:CAP], ids[2 * g + 1 : 2 * g + 2, 0:CAP]], axis=1)
        hot[:, 128 * g : 128 * g + 128] = (pick == iota((ATM, 128), 0)).astype(BF16)
    for f in range(2):
        hi, lo = split(z_rows[pl.ds(f, 16 * CAP, stride=2), :])
        z_cat[:, 128 * f : 128 * f + 128] = hi
        z_cat[:, 256 + 128 * f : 384 + 128 * f] = lo
    both = dot(hot[...], z_cat[:, 0:256]) + dot(hot[...], z_cat[:, 256:512])
    for f in range(2):
        out_g[f] = both[:, 128 * f : 128 * f + 128]

    for copy in halos + fcopies:
        copy.wait_send()

    @pl.loop(1, n_lon)
    def _(step):
        surface_copy(step).wait_send()
        partial_copy(step).wait_send()

    adjoint_out.wait()
    tracer_out.wait()


def on_device(n_lat, n_lon, tracers, cotangent, land_mask, diffusion, velocity, weights, atm_state, margins):
    fields = (2 * LEV, ROWS, COLS)
    margins = margins.reshape(3, n_lon, CAP)
    anywhere = pl.BlockSpec(memory_space=pl.ANY)
    vmem = pl.BlockSpec(memory_space=pltpu.VMEM)
    smem = pl.BlockSpec(memory_space=pltpu.SMEM)

    def buf(*shape, dtype=F32):
        return pltpu.VMEM(shape, dtype)

    dma = pltpu.SemaphoreType.DMA
    scratch = [
        buf(PLANES, XROWS, XCOLS), buf(LEV, ROWS, COLS, dtype=jnp.int32), buf(2, ATM, BLOCK), buf(WB, BLOCK, BLOCK),
        buf(20, XROWS, XCOLS), buf(2, XROWS, XCOLS), buf(2, ROWS, COLS),
        buf(HALF, 8, COLS), buf(HALF, 8, COLS), buf(ROWS, 384), buf(HALF, 8, COLS), buf(HALF, 8, COLS),
        buf(ROWS, 384), buf(ROWS, 384), buf(4, 8, 384),
        buf(2, ROWS, COLS), buf(ROWS, 128), buf(2, 8, COLS), buf(2, 8, COLS),
        buf(ROWS, 128), buf(ROWS, 128), buf(4, 8, 128),
        buf(WB // 2, 256, 256, dtype=BF16), buf(WB // 2, 256, 256, dtype=BF16), buf(2 * ATM, BLOCK),
        buf(4 * ATM, 256, dtype=BF16), buf(WB * 2 * ATM, BLOCK), buf(2 * CAP, BLOCK),
        buf(n_lon, MSG, BLOCK), buf(n_lon, MSG, BLOCK),
        buf(n_lon, MSG, BLOCK), buf(2 * BATCH * MSG, 256, dtype=BF16), buf(WB * BATCH * MSG, BLOCK),
        buf(n_lon * 2 * CAP, BLOCK), buf(n_lon * CAP, 512, dtype=BF16), buf(16, 128, dtype=jnp.int32),
        buf(ATM, n_lon * CAP, dtype=BF16),
        dma((7,)), dma((8,)), dma((8,)), dma((16,)), dma((16,)), dma((16,)), dma((16,)), dma((8,)), dma((8,)), dma((2,)),
    ]

    def body(*refs):
        kernel(n_lat, n_lon, *refs)

    out_t, out_c, out_g = pl.pallas_call(
        body,
        out_shape=(
            jax.ShapeDtypeStruct(fields, F32),
            jax.ShapeDtypeStruct(fields, F32),
            jax.ShapeDtypeStruct((2, ATM, BLOCK), F32),
        ),
        in_specs=[anywhere] * 7 + [smem, vmem],
        out_specs=(anywhere, anywhere, vmem),
        scratch_shapes=scratch,
        compiler_params=pltpu.CompilerParams(collective_id=0, has_side_effects=True, vmem_limit_bytes=48 << 20),
    )(
        tracers.reshape(fields),
        cotangent.reshape(fields),
        land_mask,
        diffusion.reshape(3 * LEV, ROWS, COLS),
        velocity.reshape(fields),
        weights,
        atm_state.reshape(2, ATM, BLOCK),
        margins,
        margins,
    )
    return out_t.reshape(tracers.shape), out_c.reshape(tracers.shape), out_g.reshape(atm_state.shape)


def solution(mesh):
    n_lat, n_lon = mesh.shape["lat"], mesh.shape["lon"]

    def run(*args):
        return on_device(n_lat, n_lon, *args)

    return jax.shard_map(
        run,
        mesh=mesh,
        in_specs=(
            P(None, None, "lat", "lon"),
            P(None, None, "lat", "lon"),
            P(None, "lat", "lon"),
            P(None, None, "lat", "lon"),
            P(None, None, "lat", "lon"),
            P(),
            P(None, "lat", "lon", None),
            P(None, "lat", "lon", None, None),
        ),
        out_specs=(
            P(None, None, "lat", "lon"),
            P(None, None, "lat", "lon"),
            P(None, "lat", "lon", None),
        ),
        check_vma=False,
    )
```

time: 626 us -> 59.7 us (0.10); the launches traced: 619 us -> 59.4 us
  matrix products: 242 us -> 0 us
  local copies, waits for them, and re-layouts: 148 us -> 9.76 us
  starting transfers between devices: 114 us -> 0 us
  other arithmetic: 90.8 us -> 0 us
  Pallas kernels: 0 us -> 49 us
  waiting for transfers between devices: 21.6 us -> 0 us
    dot_general x34 -> x0, matrix products: 242 us -> none  [the longest x16 137 us: weigh_slots(): jnp.einsum('spq,fsq->sfp', block_picks, atm_picks, precision=highest)]
    gather x48 -> x0, local copies, waits for them, and re-layouts: 126 us -> none  [the longest x16 70.3 us: weigh_slots(): block_picks = jnp.take(weights, block_ids, axis=0)]
    ppermute x36 -> x0, starting transfers between devices: 97 us -> none  [the longest x18 55.9 us: padded(): after = lax.ppermute(first, axis, down)]
    scatter-add x1 -> x0, other arithmetic: 63.8 us -> none  [on_device(): jax.ops.segment_sum(unweighed.reshape(-1, 2, BLOCK), slot_lists[1].reshap...]
    pallas_call x0 -> x1, Pallas kernels: none -> 49 us  [on_device(): pl.pallas_call(body, out_shape=(jax.ShapeDtypeStruct(fields, F32), jax.Sh...]
    ppermute x36 -> x0, waiting for transfers between devices: 21.6 us -> none  [the longest x18 13 us: padded(): after = lax.ppermute(first, axis, down)]
    all_to_all x3 -> x0, starting transfers between devices: 16.6 us -> none  [the longest x1 8.43 us: on_device(): lax.all_to_all(ocean_ids.astype(jnp.float32), 'lon', split_axis=0, concat...]
    and x32 -> x0, other arithmetic: 11.1 us -> none  [the longest x16 10.9 us: unweigh_slots(): block_picks = jnp.take(weights, block_ids, axis=0)]
  transfers between devices with their start and end apart: 39 -> 0, of which waited for: 8 -> 0; matrix products, arithmetic and copies ran while one was open for 41% -> 0% of each run, Pallas kernels for 0% -> 0%
where the time goes in v1:
time: 59.7 us; the launch traced here: 59.4 us
  Pallas kernels  49 us (82%)
  local copies, waits for them, and re-layouts  9.76 us (16%)
  between operations  0.66 us (1%)
    pallas_call x1, Pallas kernels, on_device(): pl.pallas_call(body, out_shape=(jax.ShapeDtypeStruct(fields, F32), jax.Sh...  49 us
    unnamed x19, local copies, waits for them, and re-layouts  9.76 us

profile of v1, /device:TPU:1, one launch (start us, length us, event | category | flops | bytes accessed | tf_op | source)
XLA Modules:
  0.0 59.4 jit_solution(11442294582253579638)
XLA Ops:
  0.6 0.0 copy-start
  0.6 1.6 %copy-done = f32[32,128,128]{2,1,0:T(8,128)S(1)} copy-done((f32[32,128,128]{2,1,0:T(8,128)S(1)}, f32[32,128,128]{2,1,0:T(8,128)}, u32[]{:S(2)}) %copy-start) | copy-done | bytes 2097176
  2.2 0.0 copy-start.1
  2.2 0.9 %copy-done.1 = f32[2,1,256,128]{3,2,1,0:T(8,128)S(1)} copy-done((f32[2,1,256,128]{3,2,1,0:T(8,128)S(1)}, f32[2,1,256,128]{3,2,1,0:T(8,128)}, u32[]{:S(2)}) %copy-start.1) | copy-done | bytes 262168
  3.2 0.0 copy-start.2
  3.2 0.9 %copy-done.2 = f32[3,4,16,256]{3,2,1,0:T(8,128)S(1)} copy-done((f32[3,4,16,256]{3,2,1,0:T(8,128)S(1)}, f32[3,4,16,256]{3,2,1,0:T(8,128)}, u32[]{:S(2)}) %copy-start.2) | copy-done | bytes 196632
  4.1 0.0 copy-start.3
  4.1 0.9 %copy-done.3 = f32[2,4,16,256]{3,2,1,0:T(8,128)S(1)} copy-done((f32[2,4,16,256]{3,2,1,0:T(8,128)S(1)}, f32[2,4,16,256]{3,2,1,0:T(8,128)}, u32[]{:S(2)}) %copy-start.3) | copy-done | bytes 131096
  5.0 0.0 copy-start.4
  5.0 0.9 %copy-done.4 = f32[2,4,16,256]{3,2,1,0:T(8,128)S(1)} copy-done((f32[2,4,16,256]{3,2,1,0:T(8,128)S(1)}, f32[2,4,16,256]{3,2,1,0:T(8,128)}, u32[]{:S(2)}) %copy-start.4) | copy-done | bytes 131096
  5.9 0.0 copy-start.5
  5.9 0.9 %copy-done.5 = f32[2,4,16,256]{3,2,1,0:T(8,128)S(1)} copy-done((f32[2,4,16,256]{3,2,1,0:T(8,128)S(1)}, f32[2,4,16,256]{3,2,1,0:T(8,128)}, u32[]{:S(2)}) %copy-start.5) | copy-done | bytes 131096
  6.8 0.0 copy-start.6
  6.8 0.7 %copy-done.6 = s32[3,1,1,16,64]{4,3,2,1,0:T(8,128)S(1)} copy-done((s32[3,1,1,16,64]{4,3,2,1,0:T(8,128)S(1)}, s32[3,1,1,16,64]{4,3,2,1,0:T(8,128)}, u32[]{:S(2)}) %copy-start.6) | copy-done | bytes 12312
  7.6 0.0 copy-start.7
  7.6 0.8 %copy-done.7 = s32[4,16,256]{2,1,0:T(8,128)S(1)} copy-done((s32[4,16,256]{2,1,0:T(8,128)S(1)}, s32[4,16,256]{2,1,0:T(8,128)}, u32[]{:S(2)}) %copy-start.7) | copy-done | bytes 65560
  8.4 49.0 %shard_map.103 = (f32[8,16,256]{2,1,0:T(8,128)S(1)}, f32[8,16,256]{2,1,0:T(8,128)S(1)}, f32[2,256,128]{2,1,0:T(8,128)S(1)}) custom-call(f32[8,16,256]{2,1,0:T(8,128)S(1)} %bitcast.14, f32[8,16,256]{2,1,0:T(8,128)S(1)} %bitcast.15, s32[4,16,256]{2,1,0:T(8,128)S(1)} %copy-done.7, f32[12,16,256]{2,1,0:T(8,128)S(1)} %bitcast.13, f32[8,16,256]{2,1,0:T(8,128)S(1)} %bitcast.16, ...), custom_call_target="tpu_custom_call" | custom-call | tf_op jit(solution)/shard_map/pallas_call | solution.py:463
  57.4 0.7 %copy.15 = f32[2,4,16,256]{3,2,1,0:T(8,128)} copy(f32[2,4,16,256]{3,2,1,0:T(8,128)S(1)} %bitcast.18) | data formatting | bytes 262144
  58.0 0.7 %copy.16 = f32[2,4,16,256]{3,2,1,0:T(8,128)} copy(f32[2,4,16,256]{3,2,1,0:T(8,128)S(1)} %bitcast.17) | data formatting | bytes 262144
  58.7 0.7 %copy.17 = f32[2,1,256,128]{3,2,1,0:T(8,128)} copy(f32[2,1,256,128]{3,2,1,0:T(8,128)S(1)} %bitcast.12) | data formatting | bytes 524288
Async XLA Ops:
  0.6 1.6 %copy-start = (f32[32,128,128]{2,1,0:T(8,128)S(1)}, f32[32,128,128]{2,1,0:T(8,128)}, u32[]{:S(2)}) copy-start(f32[32,128,128]{2,1,0:T(8,128)} %refs_5_.1) | copy-start | bytes 6291460
  2.2 0.9 %copy-start.1 = (f32[2,1,256,128]{3,2,1,0:T(8,128)S(1)}, f32[2,1,256,128]{3,2,1,0:T(8,128)}, u32[]{:S(2)}) copy-start(f32[2,1,256,128]{3,2,1,0:T(8,128)} %param.14) | copy-start | bytes 786436
  3.2 0.9 %copy-start.2 = (f32[3,4,16,256]{3,2,1,0:T(8,128)S(1)}, f32[3,4,16,256]{3,2,1,0:T(8,128)}, u32[]{:S(2)}) copy-start(f32[3,4,16,256]{3,2,1,0:T(8,128)} %param.11) | copy-start | bytes 589828
  4.1 0.9 %copy-start.3 = (f32[2,4,16,256]{3,2,1,0:T(8,128)S(1)}, f32[2,4,16,256]{3,2,1,0:T(8,128)}, u32[]{:S(2)}) copy-start(f32[2,4,16,256]{3,2,1,0:T(8,128)} %param.8) | copy-start | bytes 393220
  5.0 0.9 %copy-start.4 = (f32[2,4,16,256]{3,2,1,0:T(8,128)S(1)}, f32[2,4,16,256]{3,2,1,0:T(8,128)}, u32[]{:S(2)}) copy-start(f32[2,4,16,256]{3,2,1,0:T(8,128)} %param.9) | copy-start | bytes 393220
  5.9 0.9 %copy-start.5 = (f32[2,4,16,256]{3,2,1,0:T(8,128)S(1)}, f32[2,4,16,256]{3,2,1,0:T(8,128)}, u32[]{:S(2)}) copy-start(f32[2,4,16,256]{3,2,1,0:T(8,128)} %param.12) | copy-start | bytes 393220
  6.8 0.7 %copy-start.6 = (s32[3,1,1,16,64]{4,3,2,1,0:T(8,128)S(1)}, s32[3,1,1,16,64]{4,3,2,1,0:T(8,128)}, u32[]{:S(2)}) copy-start(s32[3,1,1,16,64]{4,3,2,1,0:T(8,128)} %param.15) | copy-start | bytes 36868
  7.6 0.8 %copy-start.7 = (s32[4,16,256]{2,1,0:T(8,128)S(1)}, s32[4,16,256]{2,1,0:T(8,128)}, u32[]{:S(2)}) copy-start(s32[4,16,256]{2,1,0:T(8,128)} %refs_2_.1) | copy-start | bytes 196612

commit v2 on v1

--- a/solution.py
+++ b/solution.py
@@ -62,13 +62,13 @@
 
 def kernel(
     n_lat, n_lon,
-    tracers, cotangent, land, diffusion, velocity, weights, atm, slots_s, slots_v,
+    tracers, cotangent, land, diffusion, velocity, weights, atm, margins,
     out_t, out_c, out_g,
-    ext, mask_i, atm_v, weights_v, coef, force, ssum,
+    ext, mask_i, atm_v, weights_v, slots_s, slots_v, coef, force, ssum,
     send_n, send_s, send_c, recv_n, recv_s, recv_e, recv_w, recv_d,
     fsend_r, fsend_c, frecv_n, frecv_s, frecv_e, frecv_w, frecv_d,
     w_fwd, w_rev, x_rows, x_cat, table_f, picked, p_send, p_recv,
-    s_all, v_cat, table_r, z_rows, z_cat, ids, hot,
+    s_all, v_cat, table_r, z_rows, z_cat, ids, hot, grad,
     load_sem, halo_send, halo_recv, p_ssem, p_rsem, s_ssem, s_rsem, f_send, f_recv, out_sem,
 ):
     lat, lon = lax.axis_index("lat"), lax.axis_index("lon")
@@ -81,6 +81,8 @@
         (velocity, ext.at[VEL : VEL + 8, 0:ROWS, 0:COLS]),
         (land, mask_i),
         (atm, atm_v),
+        (margins, slots_s),
+        (margins, slots_v),
         (weights, weights_v),
     ]
     loads = [pltpu.make_async_copy(a, b, load_sem.at[i]) for i, (a, b) in enumerate(loads)]
@@ -177,13 +179,36 @@
     x_cat[2 * ATM :, 0:128] = lo
     x_cat[2 * ATM :, 128:256] = lo
 
-    @pl.loop(0, WB // 2)
+    @pl.loop(0, WB // 2, unroll=8)
     def _(pair):
         both = w_fwd[pair]
         out = dot_t(x_cat[0 : 2 * ATM], both) + dot_t(x_cat[2 * ATM :], both)
         at = pl.multiple_of(pair * (4 * ATM), 4 * ATM)
         table_f[pl.ds(at, 2 * ATM), :] = out[:, 0:128]
         table_f[pl.ds(at + 2 * ATM, 2 * ATM), :] = out[:, 128:256]
+
+    def partial(step):
+        k = lax.rem(lon + step, n_lon)
+        for s in range(CAP):
+            at = slots_s[2, k, s] * (2 * ATM) + 2 * slots_s[1, k, s]
+            picked[2 * s : 2 * s + 2, :] = table_f[pl.ds(at, 2), :]
+        onehot = (slots_v[0, pl.ds(k, 1), :] == iota((OCN, CAP), 0)).astype(BF16)
+        for f in range(2):
+            hi, lo = split(picked[pl.ds(f, CAP, stride=2), :])
+            p_send[step, pl.ds(f, OCN, stride=2), :] = dot(onehot, hi) + dot(onehot, lo)
+
+    def partial_copy(step):
+        return pltpu.make_async_remote_copy(
+            src_ref=p_send.at[step], dst_ref=p_recv.at[step], send_sem=p_ssem.at[step], recv_sem=p_rsem.at[step],
+            device_id=(lat, lax.rem(lon + step, n_lon)), device_id_type=MESH,
+        )
+
+    @pl.loop(1, n_lon, unroll=5)
+    def _(step):
+        partial(step)
+        partial_copy(step).start()
+
+    partial(0)
 
     for copy in halos:
         copy.wait_recv()
@@ -297,28 +322,6 @@
     def _(step):
         surface_copy(step).start()
 
-    def partial(step):
-        k = lax.rem(lon + step, n_lon)
-        for s in range(CAP):
-            at = slots_s[2, k, s] * (2 * ATM) + 2 * slots_s[1, k, s]
-            picked[2 * s : 2 * s + 2, :] = table_f[pl.ds(at, 2), :]
-        onehot = (slots_v[0, pl.ds(k, 1), :] == iota((OCN, CAP), 0)).astype(BF16)
-        for f in range(2):
-            hi, lo = split(picked[pl.ds(f, CAP, stride=2), :])
-            p_send[step, pl.ds(f, OCN, stride=2), :] = dot(onehot, hi) + dot(onehot, lo)
-
-    def partial_copy(step):
-        return pltpu.make_async_remote_copy(
-            src_ref=p_send.at[step], dst_ref=p_recv.at[step], send_sem=p_ssem.at[step], recv_sem=p_rsem.at[step],
-            device_id=(lat, lax.rem(lon + step, n_lon)), device_id_type=MESH,
-        )
-
-    @pl.loop(1, n_lon)
-    def _(step):
-        partial(step)
-        partial_copy(step).start()
-
-    partial(0)
     retreat()
     adjoint_out = pltpu.make_async_copy(ext.at[COT : COT + 8, 0:ROWS, 0:COLS], out_c, out_sem.at[0])
     adjoint_out.start()
@@ -334,7 +337,7 @@
             v_cat[MSG * (BATCH + i) : MSG * (BATCH + i + 1), 128:256] = lo
         size = MSG * BATCH
 
-        @pl.loop(0, WB // 2)
+        @pl.loop(0, WB // 2, unroll=8)
         def _(pair):
             both = w_rev[pair]
             out = dot(v_cat[0:size], both) + dot(v_cat[size:], both)
@@ -345,10 +348,25 @@
         @pl.loop(0, BATCH)
         def _(i):
             k = lax.rem(lon + n_lon - (batch * BATCH + i), n_lon)
-            base = pl.multiple_of(k * (2 * CAP), 2 * CAP)
+            base = pl.multiple_of(i * (2 * CAP), 2 * CAP)
             for s in range(CAP):
                 at = slots_s[2, k, s] * size + i * MSG + 2 * jnp.maximum(slots_s[0, k, s], 0)
                 z_rows[pl.ds(base + 2 * s, 2), :] = table_r[pl.ds(at, 2), :]
+
+        for i in range(BATCH):
+            k = lax.rem(lon + n_lon - (batch * BATCH + i), n_lon)
+            live = slots_v[0, pl.ds(k, 1), :] >= 0
+            ids[i : i + 1, 0:CAP] = jnp.where(live, slots_v[1, pl.ds(k, 1), :], -1)
+        for g in range(BATCH // 2):
+            pick = jnp.concatenate([ids[2 * g : 2 * g + 1, 0:CAP], ids[2 * g + 1 : 2 * g + 2, 0:CAP]], axis=1)
+            hot[:, 128 * g : 128 * g + 128] = (pick == iota((ATM, 128), 0)).astype(BF16)
+        for f in range(2):
+            hi, lo = split(z_rows[pl.ds(f, BATCH * CAP, stride=2), :])
+            z_cat[:, 128 * f : 128 * f + 128] = hi
+            z_cat[:, 256 + 128 * f : 384 + 128 * f] = lo
+        part = dot(hot[...], z_cat[:, 0:256]) + dot(hot[...], z_cat[:, 256:512])
+        for f in range(2):
+            grad[f] = part[:, 128 * f : 128 * f + 128] + (grad[f] if batch else 0.0)
 
     def wait_surface(batch):
         for step in range(batch * BATCH, batch * BATCH + BATCH):
@@ -406,17 +424,8 @@
         wait_surface(batch)
         reverse(batch)
 
-    ids[:, 0:CAP] = jnp.where(slots_v[0] >= 0, slots_v[1], -1)
-    for g in range(8):
-        pick = jnp.concatenate([ids[2 * g : 2 * g + 1, 0:CAP], ids[2 * g + 1 : 2 * g + 2, 0:CAP]], axis=1)
-        hot[:, 128 * g : 128 * g + 128] = (pick == iota((ATM, 128), 0)).astype(BF16)
-    for f in range(2):
-        hi, lo = split(z_rows[pl.ds(f, 16 * CAP, stride=2), :])
-        z_cat[:, 128 * f : 128 * f + 128] = hi
-        z_cat[:, 256 + 128 * f : 384 + 128 * f] = lo
-    both = dot(hot[...], z_cat[:, 0:256]) + dot(hot[...], z_cat[:, 256:512])
-    for f in range(2):
-        out_g[f] = both[:, 128 * f : 128 * f + 128]
+    grad_out = pltpu.make_async_copy(grad, out_g, out_sem.at[2])
+    grad_out.start()
 
     for copy in halos + fcopies:
         copy.wait_send()
@@ -428,14 +437,13 @@
 
     adjoint_out.wait()
     tracer_out.wait()
+    grad_out.wait()
 
 
 def on_device(n_lat, n_lon, tracers, cotangent, land_mask, diffusion, velocity, weights, atm_state, margins):
     fields = (2 * LEV, ROWS, COLS)
     margins = margins.reshape(3, n_lon, CAP)
-    anywhere = pl.BlockSpec(memory_space=pl.ANY)
-    vmem = pl.BlockSpec(memory_space=pltpu.VMEM)
-    smem = pl.BlockSpec(memory_space=pltpu.SMEM)
+    anywhere = pl.BlockSpec(memory_space=pltpu.HBM)
 
     def buf(*shape, dtype=F32):
         return pltpu.VMEM(shape, dtype)
@@ -443,6 +451,7 @@
     dma = pltpu.SemaphoreType.DMA
     scratch = [
         buf(PLANES, XROWS, XCOLS), buf(LEV, ROWS, COLS, dtype=jnp.int32), buf(2, ATM, BLOCK), buf(WB, BLOCK, BLOCK),
+        pltpu.SMEM((3, n_lon, CAP), jnp.int32), buf(3, n_lon, CAP, dtype=jnp.int32),
         buf(20, XROWS, XCOLS), buf(2, XROWS, XCOLS), buf(2, ROWS, COLS),
         buf(HALF, 8, COLS), buf(HALF, 8, COLS), buf(ROWS, 384), buf(HALF, 8, COLS), buf(HALF, 8, COLS),
         buf(ROWS, 384), buf(ROWS, 384), buf(4, 8, 384),
@@ -452,9 +461,9 @@
         buf(4 * ATM, 256, dtype=BF16), buf(WB * 2 * ATM, BLOCK), buf(2 * CAP, BLOCK),
         buf(n_lon, MSG, BLOCK), buf(n_lon, MSG, BLOCK),
         buf(n_lon, MSG, BLOCK), buf(2 * BATCH * MSG, 256, dtype=BF16), buf(WB * BATCH * MSG, BLOCK),
-        buf(n_lon * 2 * CAP, BLOCK), buf(n_lon * CAP, 512, dtype=BF16), buf(16, 128, dtype=jnp.int32),
-        buf(ATM, n_lon * CAP, dtype=BF16),
-        dma((7,)), dma((8,)), dma((8,)), dma((16,)), dma((16,)), dma((16,)), dma((16,)), dma((8,)), dma((8,)), dma((2,)),
+        buf(BATCH * 2 * CAP, BLOCK), buf(BATCH * CAP, 512, dtype=BF16), buf(16, 128, dtype=jnp.int32),
+        buf(ATM, BATCH * CAP, dtype=BF16), buf(2, ATM, BLOCK),
+        dma((9,)), dma((8,)), dma((8,)), dma((16,)), dma((16,)), dma((16,)), dma((16,)), dma((8,)), dma((8,)), dma((3,)),
     ]
 
     def body(*refs):
@@ -467,11 +476,11 @@
             jax.ShapeDtypeStruct(fields, F32),
             jax.ShapeDtypeStruct((2, ATM, BLOCK), F32),
         ),
-        in_specs=[anywhere] * 7 + [smem, vmem],
-        out_specs=(anywhere, anywhere, vmem),
+        in_specs=[anywhere] * 8,
+        out_specs=(anywhere, anywhere, anywhere),
         scratch_shapes=scratch,
         compiler_params=pltpu.CompilerParams(collective_id=0, has_side_effects=True, vmem_limit_bytes=48 << 20),
-    )(
+    )(*(pltpu.with_memory_space_constraint(x, pltpu.HBM) for x in (
         tracers.reshape(fields),
         cotangent.reshape(fields),
         land_mask,
@@ -480,8 +489,7 @@
         weights,
         atm_state.reshape(2, ATM, BLOCK),
         margins,
-        margins,
-    )
+    )))
     return out_t.reshape(tracers.shape), out_c.reshape(tracers.shape), out_g.reshape(atm_state.shape)
 
 

time: 59.7 us -> 40.1 us (0.67)
  Pallas kernels: 49 us -> 37.3 us
  local copies, waits for them, and re-layouts: 9.76 us -> 2.01 us
    pallas_call x1, Pallas kernels: 49 us -> 37.3 us  [on_device(): pl.pallas_call(body, out_shape=(jax.ShapeDtypeStruct(fields, F32), jax.Sh...]
    unnamed x19 -> x3, local copies, waits for them, and re-layouts: 9.76 us -> 2.01 us
where the time goes in v2:
time: 40.1 us; the launch traced here: 40 us
  Pallas kernels  37.3 us (93%)
  local copies, waits for them, and re-layouts  2.01 us (5%)
  between operations  0.64 us (2%)
    pallas_call x1, Pallas kernels, on_device(): pl.pallas_call(body, out_shape=(jax.ShapeDtypeStruct(fields, F32), jax.Sh...  37.3 us
    unnamed x3, local copies, waits for them, and re-layouts  2.01 us

profile of v2, /device:TPU:1, one launch (start us, length us, event | category | flops | bytes accessed | tf_op | source)
XLA Modules:
  0.0 40.0 jit_solution(6848062308465505551)
XLA Ops:
  0.6 37.3 %shard_map.103 = (f32[8,16,256]{2,1,0:T(8,128)S(1)}, f32[8,16,256]{2,1,0:T(8,128)S(1)}, f32[2,256,128]{2,1,0:T(8,128)S(1)}) custom-call(f32[8,16,256]{2,1,0:T(8,128)} %bitcast.16, f32[8,16,256]{2,1,0:T(8,128)} %bitcast.17, s32[4,16,256]{2,1,0:T(8,128)} %refs_2_.1, f32[12,16,256]{2,1,0:T(8,128)} %bitcast.15, f32[8,16,256]{2,1,0:T(8,128)} %bitcast.18, ...), custom_call_target="tpu_custom_call" | custom-call | tf_op jit(solution)/shard_map/pallas_call | solution.py:472
  37.9 0.7 %copy.15 = f32[2,4,16,256]{3,2,1,0:T(8,128)} copy(f32[2,4,16,256]{3,2,1,0:T(8,128)S(1)} %bitcast.13) | data formatting | bytes 262144
  38.6 0.7 %copy.16 = f32[2,4,16,256]{3,2,1,0:T(8,128)} copy(f32[2,4,16,256]{3,2,1,0:T(8,128)S(1)} %bitcast.12) | data formatting | bytes 262144
  39.3 0.7 %copy.17 = f32[2,1,256,128]{3,2,1,0:T(8,128)} copy(f32[2,1,256,128]{3,2,1,0:T(8,128)S(1)} %bitcast.11) | data formatting | bytes 524288

commit v3 on v2

--- a/solution.py
+++ b/solution.py
@@ -24,6 +24,7 @@
 ATM = 256
 OCN = 32
 MSG = 2 * OCN
+PLANE_ORDER = (0, 1, 3, 2)
 BATCH = 4
 
 
@@ -68,7 +69,7 @@
     send_n, send_s, send_c, recv_n, recv_s, recv_e, recv_w, recv_d,
     fsend_r, fsend_c, frecv_n, frecv_s, frecv_e, frecv_w, frecv_d,
     w_fwd, w_rev, x_rows, x_cat, table_f, picked, p_send, p_recv,
-    s_all, v_cat, table_r, z_rows, z_cat, ids, hot, grad,
+    s_all, v_cat, table_r, z_rows, ids, hot, hot_o, grad,
     load_sem, halo_send, halo_recv, p_ssem, p_rsem, s_ssem, s_rsem, f_send, f_recv, out_sem,
 ):
     lat, lon = lax.axis_index("lat"), lax.axis_index("lon")
@@ -98,7 +99,13 @@
     def _(step):
         pl.semaphore_signal(barrier, inc=1, device_id=(lat, lax.rem(lon + step, n_lon)), device_id_type=MESH)
 
-    pl.semaphore_wait(barrier, len(peers) + n_lon - 1)
+    plane, place = lax.div(lon, 4), lax.rem(lon, 4)
+
+    def target(step):
+        return 4 * lax.rem(plane + lax.div(step, 4), 4) + lax.rem(place + lax.rem(step, 4), 4)
+
+    def source(step):
+        return 4 * lax.rem(plane + 4 - lax.div(step, 4), 4) + lax.rem(place + 4 - lax.rem(step, 4), 4)
 
     lane = iota((8, 128), 1)
     row = iota((8, 128), 0)
@@ -120,11 +127,6 @@
         return pltpu.make_async_remote_copy(
             src_ref=src, dst_ref=dst, send_sem=sems[0].at[i], recv_sem=sems[1].at[i], device_id=peer, device_id_type=MESH
         )
-
-    halo = (halo_send, halo_recv)
-    halos = [remote(send_n, recv_s, halo, 0, (up, lon)), remote(send_s, recv_n, halo, 1, (down, lon))]
-    for copy in halos:
-        copy.start()
 
     def pack_columns(plane_of, count, put):
         for tile in range(-(-count // 16)):
@@ -154,6 +156,13 @@
             remote(first, to_d.at[0], sems, base + 5, (down, left)),
         ]
 
+    pl.semaphore_wait(barrier, len(peers) + n_lon - 1)
+
+    halo = (halo_send, halo_recv)
+    halos = [remote(send_n, recv_s, halo, 0, (up, lon)), remote(send_s, recv_n, halo, 1, (down, lon))]
+    for copy in halos:
+        copy.start()
+
     columns = column_copies(send_c, recv_e, recv_w, recv_d, halo, 2)
     for copy in columns:
         copy.start()
@@ -187,20 +196,30 @@
         table_f[pl.ds(at, 2 * ATM), :] = out[:, 0:128]
         table_f[pl.ds(at + 2 * ATM, 2 * ATM), :] = out[:, 128:256]
 
+    ids[:, 0:CAP] = jnp.where(slots_v[0] >= 0, slots_v[1], -1)
+
+    @pl.loop(0, n_lon, unroll=4)
+    def _(step):
+        k = target(step)
+        onehot = (slots_v[0, pl.ds(k, 1), :] == iota((OCN, CAP), 0)).astype(BF16)
+        hot_o[step, :, 0:CAP] = onehot
+        hot_o[step, :, CAP:] = onehot
+
     def partial(step):
-        k = lax.rem(lon + step, n_lon)
+        k = target(step)
         for s in range(CAP):
             at = slots_s[2, k, s] * (2 * ATM) + 2 * slots_s[1, k, s]
             picked[2 * s : 2 * s + 2, :] = table_f[pl.ds(at, 2), :]
-        onehot = (slots_v[0, pl.ds(k, 1), :] == iota((OCN, CAP), 0)).astype(BF16)
+        terms = [split(picked[pl.ds(f, CAP, stride=2), :]) for f in range(2)]
+        rhs = jnp.concatenate([jnp.concatenate([t[i] for t in terms], axis=1) for i in range(2)], axis=0)
+        sums = dot(hot_o[step], rhs)
         for f in range(2):
-            hi, lo = split(picked[pl.ds(f, CAP, stride=2), :])
-            p_send[step, pl.ds(f, OCN, stride=2), :] = dot(onehot, hi) + dot(onehot, lo)
+            p_send[step, pl.ds(f, OCN, stride=2), :] = sums[:, 128 * f : 128 * f + 128]
 
     def partial_copy(step):
         return pltpu.make_async_remote_copy(
             src_ref=p_send.at[step], dst_ref=p_recv.at[step], send_sem=p_ssem.at[step], recv_sem=p_rsem.at[step],
-            device_id=(lat, lax.rem(lon + step, n_lon)), device_id_type=MESH,
+            device_id=(lat, target(step)), device_id_type=MESH,
         )
 
     @pl.loop(1, n_lon, unroll=5)
@@ -315,12 +334,21 @@
     def surface_copy(step):
         return pltpu.make_async_remote_copy(
             src_ref=s_all.at[lon], dst_ref=s_all.at[lon], send_sem=s_ssem.at[step], recv_sem=s_rsem.at[step],
-            device_id=(lat, lax.rem(lon + step, n_lon)), device_id_type=MESH,
+            device_id=(lat, target(step)), device_id_type=MESH,
         )
 
-    @pl.loop(1, n_lon)
-    def _(step):
-        surface_copy(step).start()
+    def send_surface(batch):
+        for step in range(BATCH * PLANE_ORDER[batch], BATCH * PLANE_ORDER[batch] + BATCH):
+            if step:
+                surface_copy(step).start()
+
+    send_surface(0)
+    send_surface(1)
+
+    for g in range(16 // 2):
+        first, second = (source(BATCH * PLANE_ORDER[2 * g // BATCH] + 2 * g % BATCH + i) for i in range(2))
+        pick = jnp.concatenate([ids[pl.ds(first, 1), 0:CAP], ids[pl.ds(second, 1), 0:CAP]], axis=1)
+        hot[:, 128 * g : 128 * g + 128] = (pick == iota((ATM, 128), 0)).astype(BF16)
 
     retreat()
     adjoint_out = pltpu.make_async_copy(ext.at[COT : COT + 8, 0:ROWS, 0:COLS], out_c, out_sem.at[0])
@@ -328,9 +356,7 @@
 
     def reverse(batch):
         for i in range(BATCH):
-            step = batch * BATCH + i
-            k = lax.rem(lon + n_lon - step, n_lon)
-            hi, lo = split(s_all[k])
+            hi, lo = split(s_all[source(BATCH * PLANE_ORDER[batch] + i)])
             v_cat[MSG * i : MSG * i + MSG, 0:128] = hi
             v_cat[MSG * i : MSG * i + MSG, 128:256] = hi
             v_cat[MSG * (BATCH + i) : MSG * (BATCH + i + 1), 0:128] = lo
@@ -347,35 +373,27 @@
 
         @pl.loop(0, BATCH)
         def _(i):
-            k = lax.rem(lon + n_lon - (batch * BATCH + i), n_lon)
+            k = source(BATCH * PLANE_ORDER[batch] + i)
             base = pl.multiple_of(i * (2 * CAP), 2 * CAP)
             for s in range(CAP):
                 at = slots_s[2, k, s] * size + i * MSG + 2 * jnp.maximum(slots_s[0, k, s], 0)
                 z_rows[pl.ds(base + 2 * s, 2), :] = table_r[pl.ds(at, 2), :]
 
-        for i in range(BATCH):
-            k = lax.rem(lon + n_lon - (batch * BATCH + i), n_lon)
-            live = slots_v[0, pl.ds(k, 1), :] >= 0
-            ids[i : i + 1, 0:CAP] = jnp.where(live, slots_v[1, pl.ds(k, 1), :], -1)
-        for g in range(BATCH // 2):
-            pick = jnp.concatenate([ids[2 * g : 2 * g + 1, 0:CAP], ids[2 * g + 1 : 2 * g + 2, 0:CAP]], axis=1)
-            hot[:, 128 * g : 128 * g + 128] = (pick == iota((ATM, 128), 0)).astype(BF16)
-        for f in range(2):
-            hi, lo = split(z_rows[pl.ds(f, BATCH * CAP, stride=2), :])
-            z_cat[:, 128 * f : 128 * f + 128] = hi
-            z_cat[:, 256 + 128 * f : 384 + 128 * f] = lo
-        part = dot(hot[...], z_cat[:, 0:256]) + dot(hot[...], z_cat[:, 256:512])
+        terms = [split(z_rows[pl.ds(f, BATCH * CAP, stride=2), :]) for f in range(2)]
+        rhs = jnp.concatenate([jnp.concatenate([t[i] for t in terms], axis=1) for i in range(2)], axis=0)
+        chosen = hot[:, BATCH * CAP * batch : BATCH * CAP * (batch + 1)]
+        part = dot(jnp.concatenate([chosen, chosen], axis=1), rhs)
         for f in range(2):
             grad[f] = part[:, 128 * f : 128 * f + 128] + (grad[f] if batch else 0.0)
 
     def wait_surface(batch):
-        for step in range(batch * BATCH, batch * BATCH + BATCH):
+        for step in range(BATCH * PLANE_ORDER[batch], BATCH * PLANE_ORDER[batch] + BATCH):
             if step:
                 surface_copy(step).wait_recv()
 
     wait_surface(0)
+    send_surface(2)
     reverse(0)
-
     total = p_send[0]
     for step in range(1, 16):
         partial_copy(step).wait_recv()
@@ -401,7 +419,16 @@
         copy.start()
 
     wait_surface(1)
+    send_surface(3)
     reverse(1)
+    wait_surface(2)
+    reverse(2)
+
+    wait_surface(3)
+    reverse(3)
+
+    grad_out = pltpu.make_async_copy(grad, out_g, out_sem.at[2])
+    grad_out.start()
 
     for copy in fcopies:
         copy.wait_recv()
@@ -420,13 +447,6 @@
     tracer_out = pltpu.make_async_copy(ext.at[TRC : TRC + 8, 0:ROWS, 0:COLS], out_t, out_sem.at[1])
     tracer_out.start()
 
-    for batch in range(2, 16 // BATCH):
-        wait_surface(batch)
-        reverse(batch)
-
-    grad_out = pltpu.make_async_copy(grad, out_g, out_sem.at[2])
-    grad_out.start()
-
     for copy in halos + fcopies:
         copy.wait_send()
 
@@ -438,6 +458,14 @@
     adjoint_out.wait()
     tracer_out.wait()
     grad_out.wait()
+
+
+def place(a, b, c, out_a, out_b, out_c, sem):
+    copies = [pltpu.make_async_copy(x, y, sem.at[i]) for i, (x, y) in enumerate(((a, out_a), (b, out_b), (c, out_c)))]
+    for copy in copies:
+        copy.start()
+    for copy in copies:
+        copy.wait()
 
 
 def on_device(n_lat, n_lon, tracers, cotangent, land_mask, diffusion, velocity, weights, atm_state, margins):
@@ -461,8 +489,8 @@
         buf(4 * ATM, 256, dtype=BF16), buf(WB * 2 * ATM, BLOCK), buf(2 * CAP, BLOCK),
         buf(n_lon, MSG, BLOCK), buf(n_lon, MSG, BLOCK),
         buf(n_lon, MSG, BLOCK), buf(2 * BATCH * MSG, 256, dtype=BF16), buf(WB * BATCH * MSG, BLOCK),
-        buf(BATCH * 2 * CAP, BLOCK), buf(BATCH * CAP, 512, dtype=BF16), buf(16, 128, dtype=jnp.int32),
-        buf(ATM, BATCH * CAP, dtype=BF16), buf(2, ATM, BLOCK),
+        buf(BATCH * 2 * CAP, BLOCK), buf(16, 128, dtype=jnp.int32),
+        buf(ATM, n_lon * CAP, dtype=BF16), buf(n_lon, OCN, 2 * CAP, dtype=BF16), buf(2, ATM, BLOCK),
         dma((9,)), dma((8,)), dma((8,)), dma((16,)), dma((16,)), dma((16,)), dma((16,)), dma((8,)), dma((8,)), dma((3,)),
     ]
 
@@ -490,6 +518,18 @@
         atm_state.reshape(2, ATM, BLOCK),
         margins,
     )))
+    out_t, out_c, out_g = pl.pallas_call(
+        place,
+        out_shape=(
+            jax.ShapeDtypeStruct(fields, F32),
+            jax.ShapeDtypeStruct(fields, F32),
+            jax.ShapeDtypeStruct((2, ATM, BLOCK), F32),
+        ),
+        in_specs=[pl.BlockSpec(memory_space=pltpu.VMEM)] * 3,
+        compiler_params=pltpu.CompilerParams(vmem_limit_bytes=2 << 20),
+        out_specs=(anywhere,) * 3,
+        scratch_shapes=[dma((3,))],
+    )(out_t, out_c, out_g)
     return out_t.reshape(tracers.shape), out_c.reshape(tracers.shape), out_g.reshape(atm_state.shape)
 
 

time: 40.1 us -> 35.5 us (0.89)
  the two profiles are of different devices: /device:TPU:1 before, /device:TPU:0 now
where the time goes in v3:
time: 35.5 us; the launch traced here: 35.3 us
  Pallas kernels  34.7 us (98%)
  between operations  0.64 us (2%)
    pallas_call x1, Pallas kernels, on_device(): pl.pallas_call(body, out_shape=(jax.ShapeDtypeStruct(fields, F32), jax.Sh...  33.9 us
    pallas_call x1, Pallas kernels, on_device(): pl.pallas_call(place, out_shape=(jax.ShapeDtypeStruct(fields, F32), jax.S...  0.82 us

profile of v3, /device:TPU:0, one launch (start us, length us, event | category | flops | bytes accessed | tf_op | source)
XLA Modules:
  0.0 35.3 jit_solution(13510885419775223533)
XLA Ops:
  0.6 33.9 %shard_map.103 = (f32[8,16,256]{2,1,0:T(8,128)S(1)}, f32[8,16,256]{2,1,0:T(8,128)S(1)}, f32[2,256,128]{2,1,0:T(8,128)S(1)}) custom-call(f32[8,16,256]{2,1,0:T(8,128)} %bitcast.13, f32[8,16,256]{2,1,0:T(8,128)} %bitcast.14, s32[4,16,256]{2,1,0:T(8,128)} %refs_2_.1, f32[12,16,256]{2,1,0:T(8,128)} %bitcast.12, f32[8,16,256]{2,1,0:T(8,128)} %bitcast.15, ...), custom_call_target="tpu_custom_call" | custom-call | tf_op jit(solution)/shard_map/pallas_call | solution.py:500
  34.5 0.8 %shard_map.104 = (f32[8,16,256]{2,1,0:T(8,128)}, f32[8,16,256]{2,1,0:T(8,128)}, f32[2,256,128]{2,1,0:T(8,128)}) custom-call(f32[8,16,256]{2,1,0:T(8,128)S(1)} %get-tuple-element.9.a, f32[8,16,256]{2,1,0:T(8,128)S(1)} %get-tuple-element.10.b, f32[2,256,128]{2,1,0:T(8,128)S(1)} %get-tuple-element.11.c), custom_call_target="tpu_custom_call" | custom-call | tf_op jit(solution)/shard_map/pallas_call | solution.py:521

commit v4 on v3

--- a/solution.py
+++ b/solution.py
@@ -65,10 +65,10 @@
     n_lat, n_lon,
     tracers, cotangent, land, diffusion, velocity, weights, atm, margins,
     out_t, out_c, out_g,
-    ext, mask_i, atm_v, weights_v, slots_s, slots_v, coef, force, ssum,
+    ext, mask_i, atm_v, weights_v, rows_s, rows_v, slots_v, coef, force, ssum,
     send_n, send_s, send_c, recv_n, recv_s, recv_e, recv_w, recv_d,
     fsend_r, fsend_c, frecv_n, frecv_s, frecv_e, frecv_w, frecv_d,
-    w_fwd, w_rev, x_rows, x_cat, table_f, picked, p_send, p_recv,
+    w_fwd, w_rev, x_rows, x_cat, table_f, picked, p_send, p_recv, q_send, q_recv,
     s_all, v_cat, table_r, z_rows, ids, hot, hot_o, grad,
     load_sem, halo_send, halo_recv, p_ssem, p_rsem, s_ssem, s_rsem, f_send, f_recv, out_sem,
 ):
@@ -81,9 +81,8 @@
         (diffusion, ext.at[DIF : DIF + 12, 0:ROWS, 0:COLS]),
         (velocity, ext.at[VEL : VEL + 8, 0:ROWS, 0:COLS]),
         (land, mask_i),
+        (margins, slots_v),
         (atm, atm_v),
-        (margins, slots_s),
-        (margins, slots_v),
         (weights, weights_v),
     ]
     loads = [pltpu.make_async_copy(a, b, load_sem.at[i]) for i, (a, b) in enumerate(loads)]
@@ -91,15 +90,19 @@
         copy.start()
 
     barrier = pltpu.get_barrier_semaphore()
-    peers = [(up, lon), (down, lon), (up, left), (up, right), (down, left), (down, right)]
+    plane, place = lax.div(lon, 4), lax.rem(lon, 4)
+
+    def in_plane(b):
+        return (lat, 4 * plane + lax.rem(place + b, 4))
+
+    def across(a):
+        return (lat, 4 * lax.rem(plane + a, 4) + place)
+
+    peers = [(up, lon), (down, lon), (up, left), (up, right), (down, left), (down, right), (lat, left), (lat, right)]
+    peers += [in_plane(i) for i in range(1, 4)] + [across(i) for i in range(1, 4)]
     for peer in peers:
         pl.semaphore_signal(barrier, inc=1, device_id=peer, device_id_type=MESH)
 
-    @pl.loop(1, n_lon)
-    def _(step):
-        pl.semaphore_signal(barrier, inc=1, device_id=(lat, lax.rem(lon + step, n_lon)), device_id_type=MESH)
-
-    plane, place = lax.div(lon, 4), lax.rem(lon, 4)
 
     def target(step):
         return 4 * lax.rem(plane + lax.div(step, 4), 4) + lax.rem(place + lax.rem(step, 4), 4)
@@ -112,7 +115,7 @@
     row2 = iota((8, COLS), 0)
     low = row2 < 4
     group = lax.rem((lane + 4) // 8, 16)
-    for copy in loads[:5]:
+    for copy in loads[:6]:
         copy.wait()
     ext[MSK : MSK + 4, 0:ROWS, 0:COLS] = mask_i[...].astype(F32)
 
@@ -127,6 +130,12 @@
         return pltpu.make_async_remote_copy(
             src_ref=src, dst_ref=dst, send_sem=sems[0].at[i], recv_sem=sems[1].at[i], device_id=peer, device_id_type=MESH
         )
+
+    ids[:, 0:CAP] = jnp.where(slots_v[0] >= 0, slots_v[1], -1)
+    rows_v[0, :, 0:CAP] = slots_v[2] * (2 * ATM) + 2 * slots_v[1]
+    rows_v[1, :, 0:CAP] = slots_v[2] * (MSG * BATCH) + 2 * jnp.maximum(slots_v[0], 0)
+    index_copy = pltpu.make_async_copy(rows_v, rows_s, load_sem.at[8])
+    index_copy.start()
 
     def pack_columns(plane_of, count, put):
         for tile in range(-(-count // 16)):
@@ -156,7 +165,7 @@
             remote(first, to_d.at[0], sems, base + 5, (down, left)),
         ]
 
-    pl.semaphore_wait(barrier, len(peers) + n_lon - 1)
+    pl.semaphore_wait(barrier, len(peers))
 
     halo = (halo_send, halo_recv)
     halos = [remote(send_n, recv_s, halo, 0, (up, lon)), remote(send_s, recv_n, halo, 1, (down, lon))]
@@ -168,8 +177,9 @@
         copy.start()
     halos += columns
 
-    for copy in loads[5:]:
+    for copy in loads[6:]:
         copy.wait()
+    index_copy.wait()
 
     @pl.loop(0, WB // 2)
     def _(pair):
@@ -196,7 +206,6 @@
         table_f[pl.ds(at, 2 * ATM), :] = out[:, 0:128]
         table_f[pl.ds(at + 2 * ATM, 2 * ATM), :] = out[:, 128:256]
 
-    ids[:, 0:CAP] = jnp.where(slots_v[0] >= 0, slots_v[1], -1)
 
     @pl.loop(0, n_lon, unroll=4)
     def _(step):
@@ -208,7 +217,7 @@
     def partial(step):
         k = target(step)
         for s in range(CAP):
-            at = slots_s[2, k, s] * (2 * ATM) + 2 * slots_s[1, k, s]
+            at = rows_s[0, k, s]
             picked[2 * s : 2 * s + 2, :] = table_f[pl.ds(at, 2), :]
         terms = [split(picked[pl.ds(f, CAP, stride=2), :]) for f in range(2)]
         rhs = jnp.concatenate([jnp.concatenate([t[i] for t in terms], axis=1) for i in range(2)], axis=0)
@@ -216,18 +225,13 @@
         for f in range(2):
             p_send[step, pl.ds(f, OCN, stride=2), :] = sums[:, 128 * f : 128 * f + 128]
 
-    def partial_copy(step):
-        return pltpu.make_async_remote_copy(
-            src_ref=p_send.at[step], dst_ref=p_recv.at[step], send_sem=p_ssem.at[step], recv_sem=p_rsem.at[step],
-            device_id=(lat, target(step)), device_id_type=MESH,
-        )
-
-    @pl.loop(1, n_lon, unroll=5)
-    def _(step):
-        partial(step)
-        partial_copy(step).start()
-
-    partial(0)
+    psem = (p_ssem, p_rsem)
+
+    partials = [remote(p_send.at[4 * a : 4 * a + 4], p_recv.at[4 * a : 4 * a + 4], psem, a - 1, across(a)) for a in range(1, 4)]
+    for a in (1, 3, 2):
+        pl.loop(4 * a, 4 * a + 4, unroll=4)(partial)
+        partials[a - 1].start()
+    pl.loop(0, 4, unroll=4)(partial)
 
     for copy in halos:
         copy.wait_recv()
@@ -331,19 +335,13 @@
         for h in range(2):
             s_all[lon, pl.ds(2 * h + f, ROWS, stride=4), :] = surface[:, 128 * h : 128 * h + 128]
 
-    def surface_copy(step):
-        return pltpu.make_async_remote_copy(
-            src_ref=s_all.at[lon], dst_ref=s_all.at[lon], send_sem=s_ssem.at[step], recv_sem=s_rsem.at[step],
-            device_id=(lat, target(step)), device_id_type=MESH,
-        )
-
-    def send_surface(batch):
-        for step in range(BATCH * PLANE_ORDER[batch], BATCH * PLANE_ORDER[batch] + BATCH):
-            if step:
-                surface_copy(step).start()
-
-    send_surface(0)
-    send_surface(1)
+    ssem = (s_ssem, s_rsem)
+    mine = s_all.at[lon]
+    row_blocks = s_all.at[pl.ds(4 * plane, 4)]
+    near = [remote(mine, mine, ssem, b - 1, in_plane(b)) for b in range(1, 4)]
+    far = [remote(row_blocks, row_blocks, ssem, 2 + a, across(a)) for a in range(1, 4)]
+    for copy in near:
+        copy.start()
 
     for g in range(16 // 2):
         first, second = (source(BATCH * PLANE_ORDER[2 * g // BATCH] + 2 * g % BATCH + i) for i in range(2))
@@ -376,7 +374,7 @@
             k = source(BATCH * PLANE_ORDER[batch] + i)
             base = pl.multiple_of(i * (2 * CAP), 2 * CAP)
             for s in range(CAP):
-                at = slots_s[2, k, s] * size + i * MSG + 2 * jnp.maximum(slots_s[0, k, s], 0)
+                at = rows_s[1, k, s] + i * MSG
                 z_rows[pl.ds(base + 2 * s, 2), :] = table_r[pl.ds(at, 2), :]
 
         terms = [split(z_rows[pl.ds(f, BATCH * CAP, stride=2), :]) for f in range(2)]
@@ -386,22 +384,29 @@
         for f in range(2):
             grad[f] = part[:, 128 * f : 128 * f + 128] + (grad[f] if batch else 0.0)
 
-    def wait_surface(batch):
-        for step in range(BATCH * PLANE_ORDER[batch], BATCH * PLANE_ORDER[batch] + BATCH):
-            if step:
-                surface_copy(step).wait_recv()
-
-    wait_surface(0)
-    send_surface(2)
+    for copy in near:
+        copy.wait_recv()
+    far[0].start()
+    far[2].start()
+
+    for copy in partials:
+        copy.wait_recv()
+    for b in range(4):
+        q_send[b] = (p_send[b] + p_recv[4 + b]) + (p_recv[8 + b] + p_recv[12 + b])
+    sums = [remote(q_send.at[b], q_recv.at[b], psem, 2 + b, in_plane(b)) for b in range(1, 4)]
+    for copy in sums:
+        copy.start()
     reverse(0)
-    total = p_send[0]
-    for step in range(1, 16):
-        partial_copy(step).wait_recv()
-        total = total + p_recv[step]
-    p_send[0] = total
+    far[1].start()
+
+    total = q_send[0]
+    for b in range(1, 4):
+        sums[b - 1].wait_recv()
+        total = total + q_recv[b]
+    q_send[0] = total
     for f in range(2):
         for h in range(2):
-            part = p_send[0, pl.ds(2 * h + f, ROWS, stride=4), :]
+            part = q_send[0, pl.ds(2 * h + f, ROWS, stride=4), :]
             force[f, 0:ROWS, 128 * h : 128 * h + 128] = part * mask0[:, 128 * h : 128 * h + 128]
         fsend_r[f] = force[f, 0:ROWS, 0:COLS]
 
@@ -418,14 +423,9 @@
     for copy in fcopies:
         copy.start()
 
-    wait_surface(1)
-    send_surface(3)
-    reverse(1)
-    wait_surface(2)
-    reverse(2)
-
-    wait_surface(3)
-    reverse(3)
+    for batch in range(1, 4):
+        far[PLANE_ORDER[batch] - 1].wait_recv()
+        reverse(batch)
 
     grad_out = pltpu.make_async_copy(grad, out_g, out_sem.at[2])
     grad_out.start()
@@ -447,14 +447,8 @@
     tracer_out = pltpu.make_async_copy(ext.at[TRC : TRC + 8, 0:ROWS, 0:COLS], out_t, out_sem.at[1])
     tracer_out.start()
 
-    for copy in halos + fcopies:
+    for copy in halos + fcopies + near + far + partials + sums:
         copy.wait_send()
-
-    @pl.loop(1, n_lon)
-    def _(step):
-        surface_copy(step).wait_send()
-        partial_copy(step).wait_send()
-
     adjoint_out.wait()
     tracer_out.wait()
     grad_out.wait()
@@ -479,7 +473,7 @@
     dma = pltpu.SemaphoreType.DMA
     scratch = [
         buf(PLANES, XROWS, XCOLS), buf(LEV, ROWS, COLS, dtype=jnp.int32), buf(2, ATM, BLOCK), buf(WB, BLOCK, BLOCK),
-        pltpu.SMEM((3, n_lon, CAP), jnp.int32), buf(3, n_lon, CAP, dtype=jnp.int32),
+        pltpu.SMEM((2, n_lon, 128), jnp.int32), buf(2, n_lon, 128, dtype=jnp.int32), buf(3, n_lon, CAP, dtype=jnp.int32),
         buf(20, XROWS, XCOLS), buf(2, XROWS, XCOLS), buf(2, ROWS, COLS),
         buf(HALF, 8, COLS), buf(HALF, 8, COLS), buf(ROWS, 384), buf(HALF, 8, COLS), buf(HALF, 8, COLS),
         buf(ROWS, 384), buf(ROWS, 384), buf(4, 8, 384),
@@ -487,11 +481,11 @@
         buf(ROWS, 128), buf(ROWS, 128), buf(4, 8, 128),
         buf(WB // 2, 256, 256, dtype=BF16), buf(WB // 2, 256, 256, dtype=BF16), buf(2 * ATM, BLOCK),
         buf(4 * ATM, 256, dtype=BF16), buf(WB * 2 * ATM, BLOCK), buf(2 * CAP, BLOCK),
-        buf(n_lon, MSG, BLOCK), buf(n_lon, MSG, BLOCK),
+        buf(n_lon, MSG, BLOCK), buf(n_lon, MSG, BLOCK), buf(4, MSG, BLOCK), buf(4, MSG, BLOCK),
         buf(n_lon, MSG, BLOCK), buf(2 * BATCH * MSG, 256, dtype=BF16), buf(WB * BATCH * MSG, BLOCK),
         buf(BATCH * 2 * CAP, BLOCK), buf(16, 128, dtype=jnp.int32),
         buf(ATM, n_lon * CAP, dtype=BF16), buf(n_lon, OCN, 2 * CAP, dtype=BF16), buf(2, ATM, BLOCK),
-        dma((9,)), dma((8,)), dma((8,)), dma((16,)), dma((16,)), dma((16,)), dma((16,)), dma((8,)), dma((8,)), dma((3,)),
+        dma((9,)), dma((8,)), dma((8,)), dma((6,)), dma((6,)), dma((6,)), dma((6,)), dma((8,)), dma((8,)), dma((3,)),
     ]
 
     def body(*refs):

time: 35.5 us -> 34.4 us (0.969)
  the two profiles are of different devices: /device:TPU:0 before, /device:TPU:27 now
where the time goes in v4:
time: 34.4 us; the launch traced here: 34.3 us
  Pallas kernels  33.6 us (98%)
  between operations  0.64 us (2%)
    pallas_call x1, Pallas kernels, on_device(): pl.pallas_call(body, out_shape=(jax.ShapeDtypeStruct(fields, F32), jax.Sh...  32.8 us
    pallas_call x1, Pallas kernels, on_device(): pl.pallas_call(place, out_shape=(jax.ShapeDtypeStruct(fields, F32), jax.S...  0.82 us

profile of v4, /device:TPU:27, one launch (start us, length us, event | category | flops | bytes accessed | tf_op | source)
XLA Modules:
  0.0 34.3 jit_solution(15400205413809377253)
XLA Ops:
  0.6 32.8 %shard_map.103 = (f32[8,16,256]{2,1,0:T(8,128)S(1)}, f32[8,16,256]{2,1,0:T(8,128)S(1)}, f32[2,256,128]{2,1,0:T(8,128)S(1)}) custom-call(f32[8,16,256]{2,1,0:T(8,128)} %bitcast.13, f32[8,16,256]{2,1,0:T(8,128)} %bitcast.14, s32[4,16,256]{2,1,0:T(8,128)} %refs_2_.1, f32[12,16,256]{2,1,0:T(8,128)} %bitcast.12, f32[8,16,256]{2,1,0:T(8,128)} %bitcast.15, ...), custom_call_target="tpu_custom_call" | custom-call | tf_op jit(solution)/shard_map/pallas_call | solution.py:494
  33.5 0.8 %shard_map.104 = (f32[8,16,256]{2,1,0:T(8,128)}, f32[8,16,256]{2,1,0:T(8,128)}, f32[2,256,128]{2,1,0:T(8,128)}) custom-call(f32[8,16,256]{2,1,0:T(8,128)S(1)} %get-tuple-element.9.a, f32[8,16,256]{2,1,0:T(8,128)S(1)} %get-tuple-element.10.b, f32[2,256,128]{2,1,0:T(8,128)S(1)} %get-tuple-element.11.c), custom_call_target="tpu_custom_call" | custom-call | tf_op jit(solution)/shard_map/pallas_call | solution.py:515

commit v5 on v4

--- a/solution.py
+++ b/solution.py
@@ -86,7 +86,7 @@
         (weights, weights_v),
     ]
     loads = [pltpu.make_async_copy(a, b, load_sem.at[i]) for i, (a, b) in enumerate(loads)]
-    for copy in loads:
+    for copy in loads[:7]:
         copy.start()
 
     barrier = pltpu.get_barrier_semaphore()
@@ -117,6 +117,7 @@
     group = lax.rem((lane + 4) // 8, 16)
     for copy in loads[:6]:
         copy.wait()
+    loads[7].start()
     ext[MSK : MSK + 4, 0:ROWS, 0:COLS] = mask_i[...].astype(F32)
 
     @pl.loop(0, HALF)
@@ -165,6 +166,14 @@
             remote(first, to_d.at[0], sems, base + 5, (down, left)),
         ]
 
+
+    @pl.loop(0, n_lon, unroll=4)
+    def _(step):
+        k = target(step)
+        onehot = (slots_v[0, pl.ds(k, 1), :] == iota((OCN, CAP), 0)).astype(BF16)
+        hot_o[step, :, 0:CAP] = onehot
+        hot_o[step, :, CAP:] = onehot
+
     pl.semaphore_wait(barrier, len(peers))
 
     halo = (halo_send, halo_recv)
@@ -205,14 +214,6 @@
         at = pl.multiple_of(pair * (4 * ATM), 4 * ATM)
         table_f[pl.ds(at, 2 * ATM), :] = out[:, 0:128]
         table_f[pl.ds(at + 2 * ATM, 2 * ATM), :] = out[:, 128:256]
-
-
-    @pl.loop(0, n_lon, unroll=4)
-    def _(step):
-        k = target(step)
-        onehot = (slots_v[0, pl.ds(k, 1), :] == iota((OCN, CAP), 0)).astype(BF16)
-        hot_o[step, :, 0:CAP] = onehot
-        hot_o[step, :, CAP:] = onehot
 
     def partial(step):
         k = target(step)
@@ -231,7 +232,6 @@
     for a in (1, 3, 2):
         pl.loop(4 * a, 4 * a + 4, unroll=4)(partial)
         partials[a - 1].start()
-    pl.loop(0, 4, unroll=4)(partial)
 
     for copy in halos:
         copy.wait_recv()
@@ -343,6 +343,8 @@
     for copy in near:
         copy.start()
 
+    pl.loop(0, 4, unroll=4)(partial)
+
     for g in range(16 // 2):
         first, second = (source(BATCH * PLANE_ORDER[2 * g // BATCH] + 2 * g % BATCH + i) for i in range(2))
         pick = jnp.concatenate([ids[pl.ds(first, 1), 0:CAP], ids[pl.ds(second, 1), 0:CAP]], axis=1)
@@ -351,6 +353,15 @@
     retreat()
     adjoint_out = pltpu.make_async_copy(ext.at[COT : COT + 8, 0:ROWS, 0:COLS], out_c, out_sem.at[0])
     adjoint_out.start()
+
+    def gather(batch):
+        count = BATCH * CAP
+        terms = [split(z_rows[pl.ds(2 * count * batch + f, count, stride=2), :]) for f in range(2)]
+        rhs = jnp.concatenate([jnp.concatenate([t[i] for t in terms], axis=1) for i in range(2)], axis=0)
+        chosen = hot[:, count * batch : count * (batch + 1)]
+        part = dot(jnp.concatenate([chosen, chosen], axis=1), rhs)
+        for f in range(2):
+            grad[f] = part[:, 128 * f : 128 * f + 128] + (grad[f] if batch else 0.0)
 
     def reverse(batch):
         for i in range(BATCH):
@@ -361,7 +372,7 @@
             v_cat[MSG * (BATCH + i) : MSG * (BATCH + i + 1), 128:256] = lo
         size = MSG * BATCH
 
-        @pl.loop(0, WB // 2, unroll=8)
+        @pl.loop(0, WB // 2, unroll=16)
         def _(pair):
             both = w_rev[pair]
             out = dot(v_cat[0:size], both) + dot(v_cat[size:], both)
@@ -369,20 +380,16 @@
             table_r[pl.ds(at, size), :] = out[:, 0:128]
             table_r[pl.ds(at + size, size), :] = out[:, 128:256]
 
-        @pl.loop(0, BATCH)
+        if batch:
+            gather(batch - 1)
+
+        @pl.loop(0, BATCH, unroll=4)
         def _(i):
             k = source(BATCH * PLANE_ORDER[batch] + i)
-            base = pl.multiple_of(i * (2 * CAP), 2 * CAP)
+            base = pl.multiple_of((batch * BATCH + i) * (2 * CAP), 2 * CAP)
             for s in range(CAP):
                 at = rows_s[1, k, s] + i * MSG
                 z_rows[pl.ds(base + 2 * s, 2), :] = table_r[pl.ds(at, 2), :]
-
-        terms = [split(z_rows[pl.ds(f, BATCH * CAP, stride=2), :]) for f in range(2)]
-        rhs = jnp.concatenate([jnp.concatenate([t[i] for t in terms], axis=1) for i in range(2)], axis=0)
-        chosen = hot[:, BATCH * CAP * batch : BATCH * CAP * (batch + 1)]
-        part = dot(jnp.concatenate([chosen, chosen], axis=1), rhs)
-        for f in range(2):
-            grad[f] = part[:, 128 * f : 128 * f + 128] + (grad[f] if batch else 0.0)
 
     for copy in near:
         copy.wait_recv()
@@ -398,7 +405,6 @@
         copy.start()
     reverse(0)
     far[1].start()
-
     total = q_send[0]
     for b in range(1, 4):
         sums[b - 1].wait_recv()
@@ -423,10 +429,14 @@
     for copy in fcopies:
         copy.start()
 
-    for batch in range(1, 4):
-        far[PLANE_ORDER[batch] - 1].wait_recv()
-        reverse(batch)
-
+    far[PLANE_ORDER[1] - 1].wait_recv()
+    reverse(1)
+    far[PLANE_ORDER[2] - 1].wait_recv()
+    reverse(2)
+    far[PLANE_ORDER[3] - 1].wait_recv()
+    reverse(3)
+
+    gather(3)
     grad_out = pltpu.make_async_copy(grad, out_g, out_sem.at[2])
     grad_out.start()
 
@@ -483,7 +493,7 @@
         buf(4 * ATM, 256, dtype=BF16), buf(WB * 2 * ATM, BLOCK), buf(2 * CAP, BLOCK),
         buf(n_lon, MSG, BLOCK), buf(n_lon, MSG, BLOCK), buf(4, MSG, BLOCK), buf(4, MSG, BLOCK),
         buf(n_lon, MSG, BLOCK), buf(2 * BATCH * MSG, 256, dtype=BF16), buf(WB * BATCH * MSG, BLOCK),
-        buf(BATCH * 2 * CAP, BLOCK), buf(16, 128, dtype=jnp.int32),
+        buf(n_lon * 2 * CAP, BLOCK), buf(16, 128, dtype=jnp.int32),
         buf(ATM, n_lon * CAP, dtype=BF16), buf(n_lon, OCN, 2 * CAP, dtype=BF16), buf(2, ATM, BLOCK),
         dma((9,)), dma((8,)), dma((8,)), dma((6,)), dma((6,)), dma((6,)), dma((6,)), dma((8,)), dma((8,)), dma((3,)),
     ]

time: 34.4 us -> 33.2 us (0.965)
  the two profiles are of different devices: /device:TPU:27 before, /device:TPU:1 now
where the time goes in v5:
time: 33.2 us; the launch traced here: 32.6 us
  Pallas kernels  31.9 us (96%)
  between operations  0.64 us (2%)
    pallas_call x1, Pallas kernels, on_device(): pl.pallas_call(body, out_shape=(jax.ShapeDtypeStruct(fields, F32), jax.Sh...  31.1 us
    pallas_call x1, Pallas kernels, on_device(): pl.pallas_call(place, out_shape=(jax.ShapeDtypeStruct(fields, F32), jax.S...  0.82 us

profile of v5, /device:TPU:1, one launch (start us, length us, event | category | flops | bytes accessed | tf_op | source)
XLA Modules:
  0.0 32.6 jit_solution(8740643600355474481)
XLA Ops:
  0.6 31.1 %shard_map.103 = (f32[8,16,256]{2,1,0:T(8,128)S(1)}, f32[8,16,256]{2,1,0:T(8,128)S(1)}, f32[2,256,128]{2,1,0:T(8,128)S(1)}) custom-call(f32[8,16,256]{2,1,0:T(8,128)} %bitcast.13, f32[8,16,256]{2,1,0:T(8,128)} %bitcast.14, s32[4,16,256]{2,1,0:T(8,128)} %refs_2_.1, f32[12,16,256]{2,1,0:T(8,128)} %bitcast.12, f32[8,16,256]{2,1,0:T(8,128)} %bitcast.15, ...), custom_call_target="tpu_custom_call" | custom-call | tf_op jit(solution)/shard_map/pallas_call | solution.py:504
  31.7 0.8 %shard_map.104 = (f32[8,16,256]{2,1,0:T(8,128)}, f32[8,16,256]{2,1,0:T(8,128)}, f32[2,256,128]{2,1,0:T(8,128)}) custom-call(f32[8,16,256]{2,1,0:T(8,128)S(1)} %get-tuple-element.9.a, f32[8,16,256]{2,1,0:T(8,128)S(1)} %get-tuple-element.10.b, f32[2,256,128]{2,1,0:T(8,128)S(1)} %get-tuple-element.11.c), custom_call_target="tpu_custom_call" | custom-call | tf_op jit(solution)/shard_map/pallas_call | solution.py:525

commit v6 on v5

--- a/solution.py
+++ b/solution.py
@@ -345,6 +345,11 @@
 
     pl.loop(0, 4, unroll=4)(partial)
 
+    for copy in near:
+        copy.wait_recv()
+    far[0].start()
+    far[2].start()
+
     for g in range(16 // 2):
         first, second = (source(BATCH * PLANE_ORDER[2 * g // BATCH] + 2 * g % BATCH + i) for i in range(2))
         pick = jnp.concatenate([ids[pl.ds(first, 1), 0:CAP], ids[pl.ds(second, 1), 0:CAP]], axis=1)
@@ -391,10 +396,6 @@
                 at = rows_s[1, k, s] + i * MSG
                 z_rows[pl.ds(base + 2 * s, 2), :] = table_r[pl.ds(at, 2), :]
 
-    for copy in near:
-        copy.wait_recv()
-    far[0].start()
-    far[2].start()
 
     for copy in partials:
         copy.wait_recv()
@@ -436,10 +437,6 @@
     far[PLANE_ORDER[3] - 1].wait_recv()
     reverse(3)
 
-    gather(3)
-    grad_out = pltpu.make_async_copy(grad, out_g, out_sem.at[2])
-    grad_out.start()
-
     for copy in fcopies:
         copy.wait_recv()
     for f in range(2):
@@ -456,6 +453,10 @@
 
     tracer_out = pltpu.make_async_copy(ext.at[TRC : TRC + 8, 0:ROWS, 0:COLS], out_t, out_sem.at[1])
     tracer_out.start()
+
+    gather(3)
+    grad_out = pltpu.make_async_copy(grad, out_g, out_sem.at[2])
+    grad_out.start()
 
     for copy in halos + fcopies + near + far + partials + sums:
         copy.wait_send()

time: 33.2 us -> 33.2 us (level)
  no operation moved by 1% of the time
where the time goes in v6:
time: 33.2 us; the launch traced here: 32.8 us
  Pallas kernels  32.2 us (97%)
  between operations  0.64 us (2%)
    pallas_call x1, Pallas kernels, on_device(): pl.pallas_call(body, out_shape=(jax.ShapeDtypeStruct(fields, F32), jax.Sh...  31.4 us
    pallas_call x1, Pallas kernels, on_device(): pl.pallas_call(place, out_shape=(jax.ShapeDtypeStruct(fields, F32), jax.S...  0.82 us

profile of v6, /device:TPU:1, one launch (start us, length us, event | category | flops | bytes accessed | tf_op | source)
XLA Modules:
  0.0 32.8 jit_solution(13204814765120496257)
XLA Ops:
  0.6 31.4 %shard_map.103 = (f32[8,16,256]{2,1,0:T(8,128)S(1)}, f32[8,16,256]{2,1,0:T(8,128)S(1)}, f32[2,256,128]{2,1,0:T(8,128)S(1)}) custom-call(f32[8,16,256]{2,1,0:T(8,128)} %bitcast.13, f32[8,16,256]{2,1,0:T(8,128)} %bitcast.14, s32[4,16,256]{2,1,0:T(8,128)} %refs_2_.1, f32[12,16,256]{2,1,0:T(8,128)} %bitcast.12, f32[8,16,256]{2,1,0:T(8,128)} %bitcast.15, ...), custom_call_target="tpu_custom_call" | custom-call | tf_op jit(solution)/shard_map/pallas_call | solution.py:505
  32.0 0.8 %shard_map.104 = (f32[8,16,256]{2,1,0:T(8,128)}, f32[8,16,256]{2,1,0:T(8,128)}, f32[2,256,128]{2,1,0:T(8,128)}) custom-call(f32[8,16,256]{2,1,0:T(8,128)S(1)} %get-tuple-element.9.a, f32[8,16,256]{2,1,0:T(8,128)S(1)} %get-tuple-element.10.b, f32[2,256,128]{2,1,0:T(8,128)S(1)} %get-tuple-element.11.c), custom_call_target="tpu_custom_call" | custom-call | tf_op jit(solution)/shard_map/pallas_call | solution.py:526
